TPU v7x, 256 devices: a whole 4x4x8 slice. The times are simulated.
256 devices in a mesh: grp: 8 (over x_hi, y), blk: 32 (over x_lo, z, core).
Axes of the slice: x: 4 (x_hi: 2, x_lo: 2; x = x_hi * 2 + x_lo), y: 4, z: 8, core: 2. Of those that a mesh axis runs over, the one named last changes fastest.
Arguments:
- queries: bfloat16 [32768, 4096], P(('grp', 'blk')), parts along dimension 0, may hold values from -256 to 256
- new_keys: bfloat16 [32768, 512], P(('grp', 'blk')), parts along dimension 0, may hold values from -6 to 6
- new_values: bfloat16 [32768, 512], P(('grp', 'blk')), parts along dimension 0, may hold values from -6 to 6
- prefix_keys: bfloat16 [32768, 512], P(('grp', 'blk')), parts along dimension 0, may hold values from -6 to 6
- prefix_values: bfloat16 [32768, 512], P(('grp', 'blk')), parts along dimension 0, may hold values from -6 to 6
- block_table: int32 [256, 16], P(('grp', 'blk')), parts along dimension 0, may hold values from 0 to 31, as said below
- prefix_blocks: int32 [256], P(('grp', 'blk')), parts along dimension 0, may hold values from 1 to 16, 320 in all
Outputs:
- attended: bfloat16 [32768, 4096], P(('grp', 'blk')), parts along dimension 0
There are 8 independent parts, one for each index of `grp`. A program takes and returns all parts, laid end to end along the dimension named above; each array names one. Nothing has to cross between parts.
Inputs may be any that keep to these rules, and one draw needn't show every extreme that they name: `block_table`: each row names 16 different prefix blocks; only the first prefix_blocks entries of a row are read. `prefix_blocks`: within each group (each index of grp) the lengths sum to 320.
All inputs are finite; a program needn't handle non-finite values.
Results may differ from a plain program's by a relative error of at most 0.008.
Values may be sent and summed in bfloat16 or wider, within the bound.
No kernel may reach another device: no remote copies, remote signals or barrier semaphores. Data moves between devices by JAX's collectives and lax.ppermute only.
A program may use at most 64 MiB of HBM per device.

v0:
```python
import functools
import math

import jax
import jax.numpy as jnp
from jax import lax
from jax.experimental import pallas as pl
from jax.experimental.pallas import tpu as pltpu
from jax.sharding import PartitionSpec as P

KVH = 4
DH = 128
BS = 128
G = 8
GW = G * DH
ROWS = G * BS
CHUNK = 4
MAXB = 16
CHUNKS = MAXB // CHUNK
MSG = GW + 3 * DH
PLANE = 4
DEPTH = 8
WAVE = 5
SCALE = DH**-0.5 * math.log2(math.e)


def index(x, z, c):
    return ((x % 2) * 8 + z % 8) * 2 + c % 2


def pairs(target):
    return [
        (index(x, z, c), index(*target(x, z, c)))
        for x in range(2)
        for z in range(8)
        for c in range(2)
    ]


AHEAD = pairs(lambda x, z, c: (x, z + 1 - 2 * c, c))
BACK = pairs(lambda x, z, c: (x, z - 1 + 2 * c, c))
SIBLING = pairs(lambda x, z, c: (x, z, c + 1))
ACROSS = pairs(lambda x, z, c: (x + 1, z, c))
DIAGONAL = pairs(lambda x, z, c: (x + 1, z, c + 1))
PEERS = (SIBLING, ACROSS, DIAGONAL)

VMEM = pl.BlockSpec(memory_space=pltpu.VMEM)
SMEM = pl.BlockSpec(memory_space=pltpu.SMEM)
ANY = pl.BlockSpec(memory_space=pl.ANY)
HBM = pl.BlockSpec(memory_space=pltpu.HBM)


def send(piece, table):
    return lax.ppermute(piece, "blk", table)


def column(start, size):
    return pl.ds(pl.multiple_of(start * size, size), size)


def peer_heads():
    me = lax.axis_index("blk")
    x, c = me // 16, me % 2
    return [2 * x + c, 2 * x + 1 - c, 2 * (1 - x) + c, 2 * (1 - x) + 1 - c]


def pack(table_ref, length_ref, pk_ref, pv_ref, q_ref, k_ref, v_ref, *refs):
    pool, request, sems = refs[:PLANE], refs[PLANE : 2 * PLANE], refs[2 * PLANE]
    copies = []

    def move(source, target):
        copies.append(pltpu.make_async_copy(source, target, sems.at[len(copies)]))
        copies[-1].start()

    heads = peer_heads()
    for j in range(PLANE):
        own = column(heads[j], DH)
        move(pk_ref.at[:, own], pool[j].at[:, :DH])
        move(pv_ref.at[:, own], pool[j].at[:, DH:])
    for j in range(PLANE):
        own = column(heads[j], DH)
        move(q_ref.at[:, column(heads[j], GW)], request[j].at[:, :GW])
        move(k_ref.at[:, own], request[j].at[:, GW : GW + DH])
        move(v_ref.at[:, own], request[j].at[:, GW + DH : GW + 2 * DH])
    lane = lax.broadcasted_iota(jnp.int32, (16, DH), 1)
    meta = jnp.where(lane == MAXB, length_ref[0], 0)
    for i in range(MAXB):
        meta = jnp.where(lane == i, table_ref[0, i], meta)
    meta = meta.astype(jnp.float32).astype(jnp.bfloat16)
    for j in range(PLANE):
        request[j][:16, GW + 2 * DH :] = meta
        request[j][16:, GW + 2 * DH :] = jnp.zeros((BS - 16, DH), jnp.bfloat16)
    for copy in copies:
        copy.wait()


def assemble(cuts, *refs):
    total = sum(cuts)
    heads = peer_heads()
    parts, out_ref, sems = refs[:total], refs[total], refs[total + 1]
    copies = []
    for j in range(PLANE):
        rows = BS // cuts[j]
        for i in range(cuts[j]):
            target = out_ref.at[i * rows : (i + 1) * rows, column(heads[j], GW)]
            at = len(copies)
            copies.append(pltpu.make_async_copy(parts[at], target, sems.at[at]))
    for copy in copies:
        copy.start()
    for copy in copies:
        copy.wait()


def attend(low, high, fresh, cuts, slot_ref, length_ref, *refs):
    n = 2
    count_pieces = high - low
    refs = list(refs)

    def take(k):
        got = refs[:k]
        del refs[:k]
        return got

    msgs, pieces = take(n), take(count_pieces)
    state = [] if fresh else take(2)
    outs = take(sum(cuts) if cuts else 2)
    kv_ref, list_ref, qs_ref, s_ref, own_ref, top_ref, acc_ref, sems = refs
    copies = [
        pltpu.make_async_copy(pieces[i], kv_ref.at[pl.ds(i * PLANE, PLANE)], sems.at[i])
        for i in range(count_pieces)
    ]
    for copy in copies:
        copy.start()
    row = lax.broadcasted_iota(jnp.int32, (ROWS, BS), 0) % BS
    causal = lax.broadcasted_iota(jnp.int32, (ROWS, BS), 1) <= row
    ones = jnp.ones((BS, DH), jnp.bfloat16)

    sizes = []
    for r in range(n):

        def pick(i, size, r=r):
            slot = slot_ref[r, i] - low * PLANE
            inside = (slot >= 0) & (slot < (high - low) * PLANE)

            @pl.when(inside)
            def _():
                list_ref[r, size] = slot

            return size + inside.astype(jnp.int32)

        sizes.append(lax.fori_loop(0, length_ref[r], pick, 0))
    count = [(size + CHUNK - 1) // CHUNK for size in sizes]

    def scores(r, keys):
        return (
            lax.dot_general(
                qs_ref[r], keys, (((1,), (1,)), ((), ())), preferred_element_type=jnp.float32
            )
            * SCALE
        )

    def begin(r):
        for h in range(G):
            qs_ref[r, h * BS : (h + 1) * BS, :] = msgs[r][:, h * DH : (h + 1) * DH]
        if fresh:
            s = jnp.where(causal, scores(r, msgs[r][:, GW : GW + DH]), -jnp.inf)
            own_ref[r] = s
            top_ref[r] = s
        else:
            top_ref[r] = state[0][r]

    def entry(r, k, j):
        at = k * CHUNK + j
        live = at < sizes[r]
        return list_ref[r, jnp.where(live, at, 0)], live

    def chunk_scores(r, k):
        keys = jnp.concatenate([kv_ref[entry(r, k, j)[0], :, :DH] for j in range(CHUNK)], axis=0)
        s = scores(r, keys)
        s_ref[r, k] = s
        top = top_ref[r]
        for j in range(CHUNK):
            top = jnp.maximum(top, s[:, j * BS : (j + 1) * BS])
        top_ref[r] = top

    def turn(r):
        top = jnp.broadcast_to(jnp.max(top_ref[r], axis=1, keepdims=True), (ROWS, BS))
        top_ref[r] = top
        if fresh:
            w = jnp.exp2(own_ref[r] - top).astype(jnp.bfloat16)
            rhs = jnp.concatenate([msgs[r][:, GW + DH : GW + 2 * DH], ones], axis=1)
            acc_ref[...] = jnp.dot(w, rhs, preferred_element_type=jnp.float32)
        else:
            acc_ref[...] = state[1][r] * jnp.tile(jnp.exp2(state[0][r] - top), (1, 2))

    def chunk_values(r, k):
        w = jnp.exp2(s_ref[r, k] - jnp.tile(top_ref[r], (1, CHUNK))).astype(jnp.bfloat16)
        rhs = []
        for j in range(CHUNK):
            slot, live = entry(r, k, j)
            both = jnp.concatenate([kv_ref[slot, :, DH:], ones], axis=1)
            rhs.append(jnp.where(live, both, jnp.zeros_like(both)))
        acc_ref[...] += jnp.dot(w, jnp.concatenate(rhs, axis=0), preferred_element_type=jnp.float32)

    def finish(r):
        if not cuts:
            outs[0][r] = top_ref[r]
            outs[1][r] = acc_ref[...]
            return
        rows = BS // cuts[r]
        for h in range(G):
            a = acc_ref[h * BS : (h + 1) * BS, :]
            a = (a[:, :DH] / a[:, DH:]).astype(jnp.bfloat16)
            for i in range(cuts[r]):
                outs[sum(cuts[:r]) + i][:, h * DH : (h + 1) * DH] = a[i * rows : (i + 1) * rows]

    begin(0)
    for copy in copies:
        copy.wait()

    @pl.loop(0, count[0])
    def _(k):
        chunk_scores(0, k)

    turn(0)
    begin(1)
    both = jnp.minimum(count[0], count[1])

    @pl.loop(0, both)
    def _(k):
        chunk_values(0, k)
        chunk_scores(1, k)

    @pl.loop(both, count[0])
    def _(k):
        chunk_values(0, k)

    @pl.loop(both, count[1])
    def _(k):
        chunk_scores(1, k)

    finish(0)
    turn(1)

    @pl.loop(0, count[1])
    def _(k):
        chunk_values(1, k)

    finish(1)


def run_attend(slots, lengths, msgs, planes, low, high, state=(), cuts=()):
    n = len(msgs)
    pieces = planes[low:high]
    chunks = min(CHUNKS, high - low)
    if cuts:
        outs = [jax.ShapeDtypeStruct((BS // cut, GW), jnp.bfloat16) for cut in cuts for _ in range(cut)]
    else:
        outs = [jax.ShapeDtypeStruct((n, ROWS, w), jnp.float32) for w in (DH, 2 * DH)]
    return pl.pallas_call(
        functools.partial(attend, low, high, not state, cuts),
        out_shape=outs,
        in_specs=[SMEM] * 2 + [VMEM] * n + [ANY] * len(pieces) + [VMEM] * len(state),
        out_specs=[VMEM] * len(outs),
        scratch_shapes=[
            pltpu.VMEM((PLANE * (high - low), BS, 2 * DH), jnp.bfloat16),
            pltpu.SMEM((n, MAXB), jnp.int32),
            pltpu.VMEM((n, ROWS, DH), jnp.bfloat16),
            pltpu.VMEM((n, chunks, ROWS, CHUNK * BS), jnp.float32),
            pltpu.VMEM((n, ROWS, BS), jnp.float32),
            pltpu.VMEM((n, ROWS, BS), jnp.float32),
            pltpu.VMEM((ROWS, 2 * DH), jnp.float32),
            pltpu.SemaphoreType.DMA((len(pieces),)),
        ],
        cost_estimate=pl.CostEstimate(flops=1, bytes_accessed=1, transcendentals=1),
        compiler_params=pltpu.CompilerParams(vmem_limit_bytes=(20 + 4 * chunks) << 20),
    )(slots, lengths, *msgs, *pieces, *state)


def body(queries, new_keys, new_values, prefix_keys, prefix_values, block_table, prefix_blocks):
    me = lax.axis_index("blk")
    x, z, c = me // 16, (me // 2) % 8, me % 2
    shards = [jax.ShapeDtypeStruct((BS, w), jnp.bfloat16) for w in (2 * DH, MSG) for _ in range(PLANE)]
    packed = pl.pallas_call(
        pack,
        out_shape=shards,
        in_specs=[SMEM] * 2 + [HBM] * 5,
        out_specs=[VMEM] * len(shards),
        scratch_shapes=[pltpu.SemaphoreType.DMA((5 * PLANE,))],
        compiler_params=pltpu.CompilerParams(vmem_limit_bytes=8 << 20),
    )(block_table, prefix_blocks, prefix_keys, prefix_values, queries, new_keys, new_values)
    pool, request = packed[:PLANE], packed[PLANE:]
    arrived = [pool[0]] + [send(o, t) for o, t in zip(pool[1:], PEERS)]
    piece = jnp.stack(arrived)
    msgs = [request[0]] + [send(o, t) for o, t in zip(request[1:], PEERS)]

    a, b = [piece], [piece]
    for _ in range(3):
        a.append(send(a[-1], AHEAD))
        b.append(send(b[-1], BACK))
    planes = [a[0], b[1], a[1], b[2], a[2], b[3], a[3]]

    info = jnp.stack([m[0, GW + 2 * DH : GW + 2 * DH + MAXB + 1] for m in msgs]).astype(jnp.int32)
    table, lengths = info[:, :MAXB], info[:, MAXB]
    deep = (((table // 2) % 8 - z) * (1 - 2 * c)) % 8
    order = jnp.where(deep < 4, jnp.maximum(2 * deep - 1, 0), jnp.minimum(2 * (8 - deep), 7))
    slots = order * 4 + (table // 16 ^ x) * 2 + (table % 2 ^ c)

    state = run_attend(slots[2:], lengths[2:], msgs[2:], planes, 0, WAVE)
    last, state = lax.optimization_barrier((a[3], state))
    planes.append(send(last, AHEAD))
    across, diagonal = run_attend(slots[2:], lengths[2:], msgs[2:], planes, WAVE, DEPTH, state, (1, 1))
    late, _ = lax.optimization_barrier((msgs[1], diagonal))
    *sibling, mine = run_attend(slots[1::-1], lengths[1::-1], [late, msgs[0]], planes, 0, DEPTH, (), (2, 1))
    parts = [
        [mine],
        [send(p, SIBLING) for p in sibling],
        [send(p, ACROSS) for p in [across]],
        [send(p, DIAGONAL) for p in [diagonal]],
    ]
    cuts = tuple(len(p) for p in parts)
    return pl.pallas_call(
        functools.partial(assemble, cuts),
        out_shape=jax.ShapeDtypeStruct(queries.shape, jnp.bfloat16),
        in_specs=[VMEM] * sum(cuts),
        out_specs=ANY,
        scratch_shapes=[pltpu.SemaphoreType.DMA((sum(cuts),))],
        compiler_params=pltpu.CompilerParams(vmem_limit_bytes=8 << 20),
    )(*[p for group in parts for p in group])


def solution(mesh):
    spec = P(("grp", "blk"), None)
    return jax.shard_map(
        body, mesh=mesh, in_specs=(spec,) * 6 + (P(("grp", "blk")),), out_specs=spec, check_vma=False
    )
```

profile of v0, /device:TPU:1, one launch (start us, length us, event | category | flops | bytes accessed | tf_op | source)
XLA Modules:
  0.0 73.2 jit_solution(10352739753479479315)
XLA Ops:
  0.7 1.2 %copy-done = bf16[128,4096]{1,0:T(8,128)(2,1)S(1)} copy-done((bf16[128,4096]{1,0:T(8,128)(2,1)S(1)}, bf16[128,4096]{1,0:T(8,128)(2,1)}, u32[]{:S(2)}) %copy-start) | copy-done | bytes 1048600
  1.9 0.9 %copy-done.1 = bf16[128,512]{1,0:T(8,128)(2,1)S(1)} copy-done((bf16[128,512]{1,0:T(8,128)(2,1)S(1)}, bf16[128,512]{1,0:T(8,128)(2,1)}, u32[]{:S(2)}) %copy-start.1) | copy-done | bytes 131096
  2.8 0.9 %copy-done.2 = bf16[128,512]{1,0:T(8,128)(2,1)S(1)} copy-done((bf16[128,512]{1,0:T(8,128)(2,1)S(1)}, bf16[128,512]{1,0:T(8,128)(2,1)}, u32[]{:S(2)}) %copy-start.2) | copy-done | bytes 131096
  3.7 0.9 %copy-done.3 = bf16[128,512]{1,0:T(8,128)(2,1)S(1)} copy-done((bf16[128,512]{1,0:T(8,128)(2,1)S(1)}, bf16[128,512]{1,0:T(8,128)(2,1)}, u32[]{:S(2)}) %copy-start.3) | copy-done | bytes 131096
  4.6 0.9 %copy-done.4 = bf16[128,512]{1,0:T(8,128)(2,1)S(1)} copy-done((bf16[128,512]{1,0:T(8,128)(2,1)S(1)}, bf16[128,512]{1,0:T(8,128)(2,1)}, u32[]{:S(2)}) %copy-start.4) | copy-done | bytes 131096
  5.5 0.7 copy-done.5
  6.2 1.7 %shard_map.73 = (bf16[128,256]{1,0:T(8,128)(2,1)S(1)}, bf16[128,256]{1,0:T(8,128)(2,1)S(1)}, bf16[128,256]{1,0:T(8,128)(2,1)S(1)}, bf16[128,256]{1,0:T(8,128)(2,...) custom-call(s32[1,16]{1,0:T(1,128)S(1)} %copy-done.5, ...), custom_call_target="tpu_custom_call" | custom-call | tf_op jit(solution)/shard_map/pallas_call | solution.py:284
  7.9 3.3 %collective-permute-start.3 = (bf16[128,256]{1,0:T(8,128)(2,1)S(1)}, bf16[128,256]{1,0:T(8,128)(2,1)S(1)}, u32[]{:S(2)}, u32[]{:S(2)}) collective-permute-start(bf16[128,256]{1,0:T(8,128)(2,1)S(1)} %get-tuple-element.29), channel_id=1, source_target_pairs={{0,1},{1,0},{2,3},{3,2},{4,5},{5,4},{6,7},{7,6},{8,9},{9,8},{10,11... | collective-permute-start | bytes 196616 | tf_op jit(solution)/shard_map/ppermute | solution.py:54
  11.2 1.7 %collective-permute-start.5 = (bf16[128,256]{1,0:T(8,128)(2,1)S(1)}, bf16[128,256]{1,0:T(8,128)(2,1)S(1)}, u32[]{:S(2)}, u32[]{:S(2)}) collective-permute-start(bf16[128,256]{1,0:T(8,128)(2,1)S(1)} %get-tuple-element.31), channel_id=1, source_target_pairs={{0,17},{1,16},{2,19},{3,18},{4,21},{5,20},{6,23},{7,22},{8,25},{9,... | collective-permute-start | bytes 196616 | tf_op jit(solution)/shard_map/ppermute | solution.py:54
  12.9 0.1 collective-permute-start
  13.1 2.0 %collective-permute-start.2 = (bf16[128,1408]{1,0:T(8,128)(2,1)S(1)}, bf16[128,1408]{1,0:T(8,128)(2,1)S(1)}, u32[]{:S(2)}, u32[]{:S(2)}) collective-permute-start(bf16[128,1408]{1,0:T(8,128)(2,1)S(1)} %get-tuple-element.27), channel_id=1, source_target_pairs={{0,17},{1,16},{2,19},{3,18},{4,21},{5,20},{6,23},{7,22},{8,25},{9,... | collective-permute-start | bytes 1081352 | tf_op jit(solution)/shard_map/ppermute | solution.py:54
  15.1 1.8 %collective-permute-done.5 = bf16[128,256]{1,0:T(8,128)(2,1)S(1)} collective-permute-done((bf16[128,256]{1,0:T(8,128)(2,1)S(1)}, bf16[128,256]{1,0:T(8,128)(2,1)S(1)}, u32[]{:S(2)}, u32[]{:S(2)}) %collective-permute-start.5) | collective-permute-done | bytes 65568 | tf_op jit(solution)/shard_map/ppermute | solution.py:54
  17.0 3.8 %collective-permute-start.9 = (bf16[4,128,256]{2,1,0:T(8,128)(2,1)S(1)}, bf16[4,128,256]{2,1,0:T(8,128)(2,1)S(1)}, u32[]{:S(2)}, u32[]{:S(2)}) collective-permute-start(bf16[4,128,256]{2,1,0:T(8,128)(2,1)S(1)} %pad_maximum_fusion.refs_2_), channel_id=1, source_target_pairs={{0,2},{1,15},{2,4},{3,1},{4,6},{5,3},{6,8},{7,5},{8,10},{9,7},{10,... | collective-permute-start | bytes 786440 | tf_op jit(solution)/shard_map/ppermute | solution.py:54
  20.8 5.6 %collective-permute-done.9.refs_4_ = bf16[4,128,256]{2,1,0:T(8,128)(2,1)S(1)} collective-permute-done((bf16[4,128,256]{2,1,0:T(8,128)(2,1)S(1)}, bf16[4,128,256]{2,1,0:T(8,128)(2,1)S(1)}, u32[]{:S(2)}, u32[]{:S(2)}) %collective-permute-start.9) | collective-permute-done | bytes 262176 | tf_op jit(solution)/shard_map/ppermute | solution.py:54
  26.3 3.4 %collective-permute-start.10 = (bf16[4,128,256]{2,1,0:T(8,128)(2,1)S(1)}, bf16[4,128,256]{2,1,0:T(8,128)(2,1)S(1)}, u32[]{:S(2)}, u32[]{:S(2)}) collective-permute-start(bf16[4,128,256]{2,1,0:T(8,128)(2,1)S(1)} %collective-permute-done.9.refs_4_), channel_id=1, source_target_pairs={{0,2},{1,15},{2,4},{3,1},{4,6},{5,3},{6,8},{7,5},{8,10},{9,7},{10,... | collective-permute-start | bytes 786440 | tf_op jit(solution)/shard_map/ppermute | solution.py:54
  29.8 2.4 %collective-permute-done.2.refs_1_ = bf16[128,1408]{1,0:T(8,128)(2,1)S(1)} collective-permute-done((bf16[128,1408]{1,0:T(8,128)(2,1)S(1)}, bf16[128,1408]{1,0:T(8,128)(2,1)S(1)}, u32[]{:S(2)}, u32[]{:S(2)}) %collective-permute-start.2) | collective-permute-done | bytes 360480 | tf_op jit(solution)/shard_map/ppermute | solution.py:54
  32.2 2.2 %collective-permute-done.10.refs_6_ = bf16[4,128,256]{2,1,0:T(8,128)(2,1)S(1)} collective-permute-done((bf16[4,128,256]{2,1,0:T(8,128)(2,1)S(1)}, bf16[4,128,256]{2,1,0:T(8,128)(2,1)S(1)}, u32[]{:S(2)}, u32[]{:S(2)}) %collective-permute-start.10) | collective-permute-done | bytes 262176 | tf_op jit(solution)/shard_map/ppermute | solution.py:54
  34.4 3.4 %collective-permute-start.11 = (bf16[4,128,256]{2,1,0:T(8,128)(2,1)S(1)}, bf16[4,128,256]{2,1,0:T(8,128)(2,1)S(1)}, u32[]{:S(2)}, u32[]{:S(2)}) collective-permute-start(bf16[4,128,256]{2,1,0:T(8,128)(2,1)S(1)} %collective-permute-done.10.refs_6_), channel_id=1, source_target_pairs={{0,2},{1,15},{2,4},{3,1},{4,6},{5,3},{6,8},{7,5},{8,10},{9,7},{10,... | collective-permute-start | bytes 786440 | tf_op jit(solution)/shard_map/ppermute | solution.py:54
  37.8 0.2 slice_reduce_fusion
  38.2 6.2 %shard_map.74 = (f32[2,1024,128]{2,1,0:T(8,128)S(1)}, f32[2,1024,256]{2,1,0:T(8,128)S(1)}) custom-call(s32[2,16]{1,0:T(2,128)S(1)} %get-tuple-element.45.slot_ref, s32[2]{0:T(128)S(1)} %get-tuple-element.43.length_ref, bf16[128,1408]{1,0:T(8,128)(2,1)S(1)} %collective-permute-done.1.refs_0_, bf16[128,1408]{1,0:T(8,128)(2,1)S(1)} %collective-permute-done.2.refs_1_, ...), custom_call_target="tpu_custom_call" | custom-call | flops 1 | bytes 1 | tf_op jit(solution)/shard_map/pallas_call | solution.py:260
  44.4 3.0 %collective-permute-start.12 = (bf16[4,128,256]{2,1,0:T(8,128)(2,1)S(1)}, bf16[4,128,256]{2,1,0:T(8,128)(2,1)S(1)}, u32[]{:S(2)}, u32[]{:S(2)}) collective-permute-start(bf16[4,128,256]{2,1,0:T(8,128)(2,1)S(1)} %collective-permute-done.11.refs_3_.refs_8_), channel_id=1, source_target_pairs={{0,2},{1,15},{2,4},{3,1},{4,6},{5,3},{6,8},{7,5},{8,10},{9,7},{10,... | collective-permute-start | bytes 786440 | tf_op jit(solution)/shard_map/ppermute | solution.py:54
  47.4 3.3 %collective-permute-done.12.refs_4_.refs_9_ = bf16[4,128,256]{2,1,0:T(8,128)(2,1)S(1)} collective-permute-done((bf16[4,128,256]{2,1,0:T(8,128)(2,1)S(1)}, bf16[4,128,256]{2,1,0:T(8,128)(2,1)S(1)}, u32[]{:S(2)}, u32[]{:S(2)}) %collective-permute-start.12) | collective-permute-done | bytes 262176 | tf_op jit(solution)/shard_map/ppermute | solution.py:54
  50.7 4.8 %shard_map.75 = (bf16[128,1024]{1,0:T(8,128)(2,1)}, bf16[128,1024]{1,0:T(8,128)(2,1)}) custom-call(s32[2,16]{1,0:T(2,128)S(1)} %get-tuple-element.45.slot_ref, s32[2]{0:T(128)S(1)} %get-tuple-element.43.length_ref, bf16[128,1408]{1,0:T(8,128)(2,1)S(1)} %collective-permute-done.1.refs_0_, bf16[128,1408]{1,0:T(8,128)(2,1)S(1)} %collective-permute-done.2.refs_1_, ...), custom_call_target="tpu_custom_call" | custom-call | flops 1 | bytes 1 | tf_op jit(solution)/shard_map/pallas_call | solution.py:260
  55.5 2.1 %collective-permute-start.15 = (bf16[128,1024]{1,0:T(8,128)(2,1)}, bf16[128,1024]{1,0:T(8,128)(2,1)S(1)}, u32[]{:S(2)}, u32[]{:S(2)}) collective-permute-start(bf16[128,1024]{1,0:T(8,128)(2,1)} %get-tuple-element.42), channel_id=1, source_target_pairs={{0,16},{1,17},{2,18},{3,19},{4,20},{5,21},{6,22},{7,23},{8,24},{9,... | collective-permute-start | bytes 786440 | tf_op jit(solution)/shard_map/ppermute | solution.py:54
  57.5 3.9 %collective-permute-start.16 = (bf16[128,1024]{1,0:T(8,128)(2,1)}, bf16[128,1024]{1,0:T(8,128)(2,1)S(1)}, u32[]{:S(2)}, u32[]{:S(2)}) collective-permute-start(bf16[128,1024]{1,0:T(8,128)(2,1)} %get-tuple-element.37), channel_id=1, source_target_pairs={{0,17},{1,16},{2,19},{3,18},{4,21},{5,20},{6,23},{7,22},{8,25},{9,... | collective-permute-start | bytes 786440 | tf_op jit(solution)/shard_map/ppermute | solution.py:54
  61.4 0.1 rev.7.length_ref
  61.5 8.8 %shard_map.76 = (bf16[64,1024]{1,0:T(8,128)(2,1)S(1)}, bf16[64,1024]{1,0:T(8,128)(2,1)S(1)}, bf16[128,1024]{1,0:T(8,128)(2,1)S(1)}) custom-call(s32[2,16]{1,0:T(2,128)S(1)} %rev.6.slot_ref, s32[2]{0:T(128)S(1)} %rev.7.length_ref, bf16[128,1408]{1,0:T(8,128)(2,1)S(1)} %collective-permute-done.refs_0_, bf16[128,1408]{1,0:T(8,128)(2,1)S(1)} %get-tuple-element.24.refs_1_, ...), custom_call_target="tpu_custom_call" | custom-call | flops 1 | bytes 1 | tf_op jit(solution)/shard_map/pallas_call | solution.py:260
  70.3 0.4 collective-permute-start.13
  70.7 0.2 collective-permute-start.14
  70.9 0.8 %collective-permute-done.13.refs_1_ = bf16[64,1024]{1,0:T(8,128)(2,1)S(1)} collective-permute-done((bf16[64,1024]{1,0:T(8,128)(2,1)S(1)}, bf16[64,1024]{1,0:T(8,128)(2,1)S(1)}, u32[]{:S(2)}, u32[]{:S(2)}) %collective-permute-start.13) | collective-permute-done | bytes 131104 | tf_op jit(solution)/shard_map/ppermute | solution.py:54
  71.7 0.3 collective-permute-done.14.refs_2_
  72.0 1.0 %shard_map.77 = bf16[128,4096]{1,0:T(8,128)(2,1)} custom-call(bf16[128,1024]{1,0:T(8,128)(2,1)S(1)} %get-tuple-element.39.refs_0_, bf16[64,1024]{1,0:T(8,128)(2,1)S(1)} %collective-permute-done.13.refs_1_, bf16[64,1024]{1,0:T(8,128)(2,1)S(1)} %collective-permute-done.14.refs_2_, bf16[128,1024]{1,0:T(8,128)(2,1)S(1)} %collective-permute-done.15.refs_3_, ...), custom_call_target="tpu_custom_call" | custom-call | tf_op jit(solution)/shard_map/pallas_call | solution.py:322
  (30 shorter events, 0.3 us)
Async XLA Ops:
  0.7 1.2 %copy-start = (bf16[128,4096]{1,0:T(8,128)(2,1)S(1)}, bf16[128,4096]{1,0:T(8,128)(2,1)}, u32[]{:S(2)}) copy-start(bf16[128,4096]{1,0:T(8,128)(2,1)} %q_ref.1) | copy-start | bytes 3145732
  1.9 0.9 %copy-start.1 = (bf16[128,512]{1,0:T(8,128)(2,1)S(1)}, bf16[128,512]{1,0:T(8,128)(2,1)}, u32[]{:S(2)}) copy-start(bf16[128,512]{1,0:T(8,128)(2,1)} %pk_ref.1) | copy-start | bytes 393220
  2.8 0.9 %copy-start.2 = (bf16[128,512]{1,0:T(8,128)(2,1)S(1)}, bf16[128,512]{1,0:T(8,128)(2,1)}, u32[]{:S(2)}) copy-start(bf16[128,512]{1,0:T(8,128)(2,1)} %pv_ref.1) | copy-start | bytes 393220
  3.7 0.9 %copy-start.3 = (bf16[128,512]{1,0:T(8,128)(2,1)S(1)}, bf16[128,512]{1,0:T(8,128)(2,1)}, u32[]{:S(2)}) copy-start(bf16[128,512]{1,0:T(8,128)(2,1)} %k_ref.1) | copy-start | bytes 393220
  4.6 0.9 %copy-start.4 = (bf16[128,512]{1,0:T(8,128)(2,1)S(1)}, bf16[128,512]{1,0:T(8,128)(2,1)}, u32[]{:S(2)}) copy-start(bf16[128,512]{1,0:T(8,128)(2,1)} %v_ref.1) | copy-start | bytes 393220
  5.5 0.7 copy-start.5
  7.9 5.2 %collective-permute-start.3 = (bf16[128,256]{1,0:T(8,128)(2,1)S(1)}, bf16[128,256]{1,0:T(8,128)(2,1)S(1)}, u32[]{:S(2)}, u32[]{:S(2)}) collective-permute-start(bf16[128,256]{1,0:T(8,128)(2,1)S(1)} %get-tuple-element.29), channel_id=1, source_target_pairs={{0,1},{1,0},{2,3},{3,2},{4,5},{5,4},{6,7},{7,6},{8,9},{9,8},{10,11... | collective-permute-start | bytes 196616 | tf_op jit(solution)/shard_map/ppermute | solution.py:54
  11.2 3.9 %collective-permute-start.4 = (bf16[128,256]{1,0:T(8,128)(2,1)S(1)}, bf16[128,256]{1,0:T(8,128)(2,1)S(1)}, u32[]{:S(2)}, u32[]{:S(2)}) collective-permute-start(bf16[128,256]{1,0:T(8,128)(2,1)S(1)} %get-tuple-element.30), channel_id=1, source_target_pairs={{0,16},{1,17},{2,18},{3,19},{4,20},{5,21},{6,22},{7,23},{8,24},{9,... | collective-permute-start | bytes 196616 | tf_op jit(solution)/shard_map/ppermute | solution.py:54
  11.2 5.7 %collective-permute-start.5 = (bf16[128,256]{1,0:T(8,128)(2,1)S(1)}, bf16[128,256]{1,0:T(8,128)(2,1)S(1)}, u32[]{:S(2)}, u32[]{:S(2)}) collective-permute-start(bf16[128,256]{1,0:T(8,128)(2,1)S(1)} %get-tuple-element.31), channel_id=1, source_target_pairs={{0,17},{1,16},{2,19},{3,18},{4,21},{5,20},{6,23},{7,22},{8,25},{9,... | collective-permute-start | bytes 196616 | tf_op jit(solution)/shard_map/ppermute | solution.py:54
  12.9 16.8 %collective-permute-start = (bf16[128,1408]{1,0:T(8,128)(2,1)}, bf16[128,1408]{1,0:T(8,128)(2,1)S(1)}, u32[]{:S(2)}, u32[]{:S(2)}) collective-permute-start(bf16[128,1408]{1,0:T(8,128)(2,1)} %get-tuple-element.25), channel_id=1, source_target_pairs={{0,1},{1,0},{2,3},{3,2},{4,5},{5,4},{6,7},{7,6},{8,9},{9,8},{10,11... | collective-permute-start | bytes 1081352 | tf_op jit(solution)/shard_map/ppermute | solution.py:54
  13.1 16.7 %collective-permute-start.1 = (bf16[128,1408]{1,0:T(8,128)(2,1)S(1)}, bf16[128,1408]{1,0:T(8,128)(2,1)S(1)}, u32[]{:S(2)}, u32[]{:S(2)}) collective-permute-start(bf16[128,1408]{1,0:T(8,128)(2,1)S(1)} %get-tuple-element.26), channel_id=1, source_target_pairs={{0,16},{1,17},{2,18},{3,19},{4,20},{5,21},{6,22},{7,23},{8,24},{9,... | collective-permute-start | bytes 1081352 | tf_op jit(solution)/shard_map/ppermute | solution.py:54
  13.1 19.1 %collective-permute-start.2 = (bf16[128,1408]{1,0:T(8,128)(2,1)S(1)}, bf16[128,1408]{1,0:T(8,128)(2,1)S(1)}, u32[]{:S(2)}, u32[]{:S(2)}) collective-permute-start(bf16[128,1408]{1,0:T(8,128)(2,1)S(1)} %get-tuple-element.27), channel_id=1, source_target_pairs={{0,17},{1,16},{2,19},{3,18},{4,21},{5,20},{6,23},{7,22},{8,25},{9,... | collective-permute-start | bytes 1081352 | tf_op jit(solution)/shard_map/ppermute | solution.py:54
  17.0 9.4 %collective-permute-start.9 = (bf16[4,128,256]{2,1,0:T(8,128)(2,1)S(1)}, bf16[4,128,256]{2,1,0:T(8,128)(2,1)S(1)}, u32[]{:S(2)}, u32[]{:S(2)}) collective-permute-start(bf16[4,128,256]{2,1,0:T(8,128)(2,1)S(1)} %pad_maximum_fusion.refs_2_), channel_id=1, source_target_pairs={{0,2},{1,15},{2,4},{3,1},{4,6},{5,3},{6,8},{7,5},{8,10},{9,7},{10,... | collective-permute-start | bytes 786440 | tf_op jit(solution)/shard_map/ppermute | solution.py:54
  20.8 9.0 %collective-permute-start.6 = (bf16[4,128,256]{2,1,0:T(8,128)(2,1)S(1)}, bf16[4,128,256]{2,1,0:T(8,128)(2,1)S(1)}, u32[]{:S(2)}, u32[]{:S(2)}) collective-permute-start(bf16[4,128,256]{2,1,0:T(8,128)(2,1)S(1)} %pad_maximum_fusion.refs_2_), channel_id=1, source_target_pairs={{0,14},{1,3},{2,0},{3,5},{4,2},{5,7},{6,4},{7,9},{8,6},{9,11},{10,... | collective-permute-start | bytes 786440 | tf_op jit(solution)/shard_map/ppermute | solution.py:54
  26.3 8.1 %collective-permute-start.10 = (bf16[4,128,256]{2,1,0:T(8,128)(2,1)S(1)}, bf16[4,128,256]{2,1,0:T(8,128)(2,1)S(1)}, u32[]{:S(2)}, u32[]{:S(2)}) collective-permute-start(bf16[4,128,256]{2,1,0:T(8,128)(2,1)S(1)} %collective-permute-done.9.refs_4_), channel_id=1, source_target_pairs={{0,2},{1,15},{2,4},{3,1},{4,6},{5,3},{6,8},{7,5},{8,10},{9,7},{10,... | collective-permute-start | bytes 786440 | tf_op jit(solution)/shard_map/ppermute | solution.py:54
  29.8 8.3 %collective-permute-start.7 = (bf16[4,128,256]{2,1,0:T(8,128)(2,1)S(1)}, bf16[4,128,256]{2,1,0:T(8,128)(2,1)S(1)}, u32[]{:S(2)}, u32[]{:S(2)}) collective-permute-start(bf16[4,128,256]{2,1,0:T(8,128)(2,1)S(1)} %collective-permute-done.6.refs_3_), channel_id=1, source_target_pairs={{0,14},{1,3},{2,0},{3,5},{4,2},{5,7},{6,4},{7,9},{8,6},{9,11},{10,... | collective-permute-start | bytes 786440 | tf_op jit(solution)/shard_map/ppermute | solution.py:54
  34.4 10.0 %collective-permute-start.11 = (bf16[4,128,256]{2,1,0:T(8,128)(2,1)S(1)}, bf16[4,128,256]{2,1,0:T(8,128)(2,1)S(1)}, u32[]{:S(2)}, u32[]{:S(2)}) collective-permute-start(bf16[4,128,256]{2,1,0:T(8,128)(2,1)S(1)} %collective-permute-done.10.refs_6_), channel_id=1, source_target_pairs={{0,2},{1,15},{2,4},{3,1},{4,6},{5,3},{6,8},{7,5},{8,10},{9,7},{10,... | collective-permute-start | bytes 786440 | tf_op jit(solution)/shard_map/ppermute | solution.py:54
  38.1 9.3 %collective-permute-start.8 = (bf16[4,128,256]{2,1,0:T(8,128)(2,1)S(1)}, bf16[4,128,256]{2,1,0:T(8,128)(2,1)S(1)}, u32[]{:S(2)}, u32[]{:S(2)}) collective-permute-start(bf16[4,128,256]{2,1,0:T(8,128)(2,1)S(1)} %collective-permute-done.7.refs_5_), channel_id=1, source_target_pairs={{0,14},{1,3},{2,0},{3,5},{4,2},{5,7},{6,4},{7,9},{8,6},{9,11},{10,... | collective-permute-start | bytes 786440 | tf_op jit(solution)/shard_map/ppermute | solution.py:54
  44.4 6.3 %collective-permute-start.12 = (bf16[4,128,256]{2,1,0:T(8,128)(2,1)S(1)}, bf16[4,128,256]{2,1,0:T(8,128)(2,1)S(1)}, u32[]{:S(2)}, u32[]{:S(2)}) collective-permute-start(bf16[4,128,256]{2,1,0:T(8,128)(2,1)S(1)} %collective-permute-done.11.refs_3_.refs_8_), channel_id=1, source_target_pairs={{0,2},{1,15},{2,4},{3,1},{4,6},{5,3},{6,8},{7,5},{8,10},{9,7},{10,... | collective-permute-start | bytes 786440 | tf_op jit(solution)/shard_map/ppermute | solution.py:54
  55.5 16.6 %collective-permute-start.15 = (bf16[128,1024]{1,0:T(8,128)(2,1)}, bf16[128,1024]{1,0:T(8,128)(2,1)S(1)}, u32[]{:S(2)}, u32[]{:S(2)}) collective-permute-start(bf16[128,1024]{1,0:T(8,128)(2,1)} %get-tuple-element.42), channel_id=1, source_target_pairs={{0,16},{1,17},{2,18},{3,19},{4,20},{5,21},{6,22},{7,23},{8,24},{9,... | collective-permute-start | bytes 786440 | tf_op jit(solution)/shard_map/ppermute | solution.py:54
  57.5 14.5 %collective-permute-start.16 = (bf16[128,1024]{1,0:T(8,128)(2,1)}, bf16[128,1024]{1,0:T(8,128)(2,1)S(1)}, u32[]{:S(2)}, u32[]{:S(2)}) collective-permute-start(bf16[128,1024]{1,0:T(8,128)(2,1)} %get-tuple-element.37), channel_id=1, source_target_pairs={{0,17},{1,16},{2,19},{3,18},{4,21},{5,20},{6,23},{7,22},{8,25},{9,... | collective-permute-start | bytes 786440 | tf_op jit(solution)/shard_map/ppermute | solution.py:54
  70.3 1.4 %collective-permute-start.13 = (bf16[64,1024]{1,0:T(8,128)(2,1)S(1)}, bf16[64,1024]{1,0:T(8,128)(2,1)S(1)}, u32[]{:S(2)}, u32[]{:S(2)}) collective-permute-start(bf16[64,1024]{1,0:T(8,128)(2,1)S(1)} %get-tuple-element.40), channel_id=1, source_target_pairs={{0,1},{1,0},{2,3},{3,2},{4,5},{5,4},{6,7},{7,6},{8,9},{9,8},{10,11... | collective-permute-start | bytes 393224 | tf_op jit(solution)/shard_map/ppermute | solution.py:54
  70.7 1.3 %collective-permute-start.14 = (bf16[64,1024]{1,0:T(8,128)(2,1)S(1)}, bf16[64,1024]{1,0:T(8,128)(2,1)S(1)}, u32[]{:S(2)}, u32[]{:S(2)}) collective-permute-start(bf16[64,1024]{1,0:T(8,128)(2,1)S(1)} %get-tuple-element.41), channel_id=1, source_target_pairs={{0,1},{1,0},{2,3},{3,2},{4,5},{5,4},{6,7},{7,6},{8,9},{9,8},{10,11... | collective-permute-start | bytes 393224 | tf_op jit(solution)/shard_map/ppermute | solution.py:54
where the time goes:
time: 72.8 us; the launch traced here: 73.2 us
  starting transfers between devices  27.4 us (38%)
  Pallas kernels  22.5 us (31%)
  waiting for transfers between devices  16.4 us (23%)
  local copies, waits for them, and re-layouts  5.83 us (8%)
  between operations  0.94 us (1%)
    ppermute x17, starting transfers between devices, send(): return lax.ppermute(piece, 'blk', table)  27.4 us
    pallas_call x3, Pallas kernels, run_attend(): pl.pallas_call(functools.partial(attend, low, high, not state, cuts), out...  19.8 us
    ppermute x17, waiting for transfers between devices, send(): return lax.ppermute(piece, 'blk', table)  16.4 us
    unnamed x12, local copies, waits for them, and re-layouts  5.49 us
    pallas_call x1, Pallas kernels, body(): pl.pallas_call(pack, out_shape=shards, in_specs=[SMEM] * 2 + [HBM] * 5, o...  1.71 us
  transfers between devices with their start and end apart: 17, of which 7 were waited for; matrix products, arithmetic and copies ran while one was open for 1% of the time, Pallas kernels for 21%

commit v1 on v0

--- a/solution.py
+++ b/solution.py
@@ -287,7 +287,6 @@
         in_specs=[SMEM] * 2 + [HBM] * 5,
         out_specs=[VMEM] * len(shards),
         scratch_shapes=[pltpu.SemaphoreType.DMA((5 * PLANE,))],
-        compiler_params=pltpu.CompilerParams(vmem_limit_bytes=8 << 20),
     )(block_table, prefix_blocks, prefix_keys, prefix_values, queries, new_keys, new_values)
     pool, request = packed[:PLANE], packed[PLANE:]
     arrived = [pool[0]] + [send(o, t) for o, t in zip(pool[1:], PEERS)]
@@ -309,7 +308,8 @@
     state = run_attend(slots[2:], lengths[2:], msgs[2:], planes, 0, WAVE)
     last, state = lax.optimization_barrier((a[3], state))
     planes.append(send(last, AHEAD))
-    across, diagonal = run_attend(slots[2:], lengths[2:], msgs[2:], planes, WAVE, DEPTH, state, (1, 1))
+    state = run_attend(slots[2:], lengths[2:], msgs[2:], planes, WAVE, DEPTH - 1, state)
+    across, diagonal = run_attend(slots[2:], lengths[2:], msgs[2:], planes, DEPTH - 1, DEPTH, state, (1, 1))
     late, _ = lax.optimization_barrier((msgs[1], diagonal))
     *sibling, mine = run_attend(slots[1::-1], lengths[1::-1], [late, msgs[0]], planes, 0, DEPTH, (), (2, 1))
     parts = [

time: 72.8 us -> 70.8 us (0.973)
  the two profiles are of different devices: /device:TPU:1 before, /device:TPU:9 now
where the time goes in v1:
time: 70.8 us; the launch traced here: 70.1 us
  starting transfers between devices  28 us (40%)
  Pallas kernels  25.8 us (36%)
  waiting for transfers between devices  13.4 us (19%)
  local copies, waits for them, and re-layouts  1.03 us (1%)
  between operations  0.94 us (1%)
  other arithmetic  0.92 us (1%)
    ppermute x17, starting transfers between devices, send(): return lax.ppermute(piece, 'blk', table)  28 us
    pallas_call x4, Pallas kernels, run_attend(): pl.pallas_call(functools.partial(attend, low, high, not state, cuts), out...  21.3 us
    ppermute x17, waiting for transfers between devices, send(): return lax.ppermute(piece, 'blk', table)  13.4 us
    pallas_call x1, Pallas kernels, body(): pl.pallas_call(pack, out_shape=shards, in_specs=[SMEM] * 2 + [HBM] * 5, o...  3.46 us
  transfers between devices with their start and end apart: 17, of which 8 were waited for; matrix products, arithmetic and copies ran while one was open for 3% of the time, Pallas kernels for 25%

profile of v1, /device:TPU:9, one launch (start us, length us, event | category | flops | bytes accessed | tf_op | source)
XLA Modules:
  0.0 70.1 jit_solution(16089900318024440927)
XLA Ops:
  0.7 3.5 %shard_map.73 = (bf16[128,256]{1,0:T(8,128)(2,1)}, bf16[128,256]{1,0:T(8,128)(2,1)}, bf16[128,256]{1,0:T(8,128)(2,1)}, bf16[128,256]{1,0:T(8,128)(2,1)}, bf16[12...) custom-call(s32[1,16]{1,0:T(1,128)} %table_ref.1, ...), custom_call_target="tpu_custom_call" | custom-call | tf_op jit(solution)/shard_map/pallas_call | solution.py:284
  4.1 0.8 %collective-permute-start.3 = (bf16[128,256]{1,0:T(8,128)(2,1)}, bf16[128,256]{1,0:T(8,128)(2,1)S(1)}, u32[]{:S(2)}, u32[]{:S(2)}) collective-permute-start(bf16[128,256]{1,0:T(8,128)(2,1)} %get-tuple-element.31), channel_id=1, source_target_pairs={{0,1},{1,0},{2,3},{3,2},{4,5},{5,4},{6,7},{7,6},{8,9},{9,8},{10,11... | collective-permute-start | bytes 196616 | tf_op jit(solution)/shard_map/ppermute | solution.py:54
  4.9 1.2 %collective-permute-start.4 = (bf16[128,256]{1,0:T(8,128)(2,1)}, bf16[128,256]{1,0:T(8,128)(2,1)S(1)}, u32[]{:S(2)}, u32[]{:S(2)}) collective-permute-start(bf16[128,256]{1,0:T(8,128)(2,1)} %get-tuple-element.32), channel_id=1, source_target_pairs={{0,16},{1,17},{2,18},{3,19},{4,20},{5,21},{6,22},{7,23},{8,24},{9,... | collective-permute-start | bytes 196616 | tf_op jit(solution)/shard_map/ppermute | solution.py:54
  6.1 0.5 collective-permute-start.5
  6.6 1.2 %collective-permute-start.1 = (bf16[128,1408]{1,0:T(8,128)(2,1)}, bf16[128,1408]{1,0:T(8,128)(2,1)S(1)}, u32[]{:S(2)}, u32[]{:S(2)}) collective-permute-start(bf16[128,1408]{1,0:T(8,128)(2,1)} %get-tuple-element.28), channel_id=1, source_target_pairs={{0,16},{1,17},{2,18},{3,19},{4,20},{5,21},{6,22},{7,23},{8,24},{9,... | collective-permute-start | bytes 1081352 | tf_op jit(solution)/shard_map/ppermute | solution.py:54
  7.8 0.6 collective-permute-start.2
  8.5 0.3 collective-permute-done.4
  8.7 2.0 %collective-permute-done.5 = bf16[128,256]{1,0:T(8,128)(2,1)S(1)} collective-permute-done((bf16[128,256]{1,0:T(8,128)(2,1)}, bf16[128,256]{1,0:T(8,128)(2,1)S(1)}, u32[]{:S(2)}, u32[]{:S(2)}) %collective-permute-start.5) | collective-permute-done | bytes 65568 | tf_op jit(solution)/shard_map/ppermute | solution.py:54
  10.7 0.9 %pad_maximum_fusion.refs_2_ = bf16[4,128,256]{2,1,0:T(8,128)(2,1)S(1)} fusion(bf16[1,128,256]{2,1,0:T(8,128)(2,1)S(1)} %bitcast.7, bf16[1,128,256]{2,1,0:T(8,128)(2,1)S(1)} %bitcast.6, bf16[1,128,256]{2,1,0:T(8,128)(2,1)S(1)} %bitcast.5, bf16[1,128,256]{2,1,0:T(8,128)(2,1)} %bitcast.4), kind=kLoop, calls=%fused_computation | loop fusion | flops 393216 | bytes 524288 | tf_op jit(solution)/shard_map/stack | solution.py:293
  11.6 1.7 %collective-permute-start.9 = (bf16[4,128,256]{2,1,0:T(8,128)(2,1)S(1)}, bf16[4,128,256]{2,1,0:T(8,128)(2,1)S(1)}, u32[]{:S(2)}, u32[]{:S(2)}) collective-permute-start(bf16[4,128,256]{2,1,0:T(8,128)(2,1)S(1)} %pad_maximum_fusion.refs_2_), channel_id=1, source_target_pairs={{0,14},{1,3},{2,0},{3,5},{4,2},{5,7},{6,4},{7,9},{8,6},{9,11},{10,... | collective-permute-start | bytes 786440 | tf_op jit(solution)/shard_map/ppermute | solution.py:54
  13.3 4.0 %collective-permute-start.6 = (bf16[4,128,256]{2,1,0:T(8,128)(2,1)S(1)}, bf16[4,128,256]{2,1,0:T(8,128)(2,1)S(1)}, u32[]{:S(2)}, u32[]{:S(2)}) collective-permute-start(bf16[4,128,256]{2,1,0:T(8,128)(2,1)S(1)} %pad_maximum_fusion.refs_2_), channel_id=1, source_target_pairs={{0,2},{1,15},{2,4},{3,1},{4,6},{5,3},{6,8},{7,5},{8,10},{9,7},{10,... | collective-permute-start | bytes 786440 | tf_op jit(solution)/shard_map/ppermute | solution.py:54
  17.3 0.7 slice.40
  18.0 3.0 %collective-permute-done.9.refs_3_ = bf16[4,128,256]{2,1,0:T(8,128)(2,1)S(1)} collective-permute-done((bf16[4,128,256]{2,1,0:T(8,128)(2,1)S(1)}, bf16[4,128,256]{2,1,0:T(8,128)(2,1)S(1)}, u32[]{:S(2)}, u32[]{:S(2)}) %collective-permute-start.9) | collective-permute-done | bytes 262176 | tf_op jit(solution)/shard_map/ppermute | solution.py:54
  21.0 2.1 %collective-permute-done.6.refs_4_ = bf16[4,128,256]{2,1,0:T(8,128)(2,1)S(1)} collective-permute-done((bf16[4,128,256]{2,1,0:T(8,128)(2,1)S(1)}, bf16[4,128,256]{2,1,0:T(8,128)(2,1)S(1)}, u32[]{:S(2)}, u32[]{:S(2)}) %collective-permute-start.6) | collective-permute-done | bytes 262176 | tf_op jit(solution)/shard_map/ppermute | solution.py:54
  23.1 3.4 %collective-permute-start.7 = (bf16[4,128,256]{2,1,0:T(8,128)(2,1)S(1)}, bf16[4,128,256]{2,1,0:T(8,128)(2,1)S(1)}, u32[]{:S(2)}, u32[]{:S(2)}) collective-permute-start(bf16[4,128,256]{2,1,0:T(8,128)(2,1)S(1)} %collective-permute-done.6.refs_4_), channel_id=1, source_target_pairs={{0,2},{1,15},{2,4},{3,1},{4,6},{5,3},{6,8},{7,5},{8,10},{9,7},{10,... | collective-permute-start | bytes 786440 | tf_op jit(solution)/shard_map/ppermute | solution.py:54
  26.6 4.8 %collective-permute-done.7.refs_6_ = bf16[4,128,256]{2,1,0:T(8,128)(2,1)S(1)} collective-permute-done((bf16[4,128,256]{2,1,0:T(8,128)(2,1)S(1)}, bf16[4,128,256]{2,1,0:T(8,128)(2,1)S(1)}, u32[]{:S(2)}, u32[]{:S(2)}) %collective-permute-start.7) | collective-permute-done | bytes 262176 | tf_op jit(solution)/shard_map/ppermute | solution.py:54
  31.5 3.4 %collective-permute-start.8 = (bf16[4,128,256]{2,1,0:T(8,128)(2,1)S(1)}, bf16[4,128,256]{2,1,0:T(8,128)(2,1)S(1)}, u32[]{:S(2)}, u32[]{:S(2)}) collective-permute-start(bf16[4,128,256]{2,1,0:T(8,128)(2,1)S(1)} %collective-permute-done.7.refs_6_), channel_id=1, source_target_pairs={{0,2},{1,15},{2,4},{3,1},{4,6},{5,3},{6,8},{7,5},{8,10},{9,7},{10,... | collective-permute-start | bytes 786440 | tf_op jit(solution)/shard_map/ppermute | solution.py:54
  34.9 0.2 slice_reduce_fusion
  35.2 5.5 %shard_map.74 = (f32[2,1024,128]{2,1,0:T(8,128)S(1)}, f32[2,1024,256]{2,1,0:T(8,128)S(1)}) custom-call(s32[2,16]{1,0:T(2,128)S(1)} %get-tuple-element.49.slot_ref, s32[2]{0:T(128)S(1)} %get-tuple-element.47.length_ref, bf16[128,1408]{1,0:T(8,128)(2,1)S(1)} %collective-permute-done.1.refs_0_, bf16[128,1408]{1,0:T(8,128)(2,1)S(1)} %collective-permute-done.2.refs_1_, ...), custom_call_target="tpu_custom_call" | custom-call | flops 1 | bytes 1 | tf_op jit(solution)/shard_map/pallas_call | solution.py:260
  40.8 3.7 %collective-permute-start.11 = (bf16[4,128,256]{2,1,0:T(8,128)(2,1)S(1)}, bf16[4,128,256]{2,1,0:T(8,128)(2,1)S(1)}, u32[]{:S(2)}, u32[]{:S(2)}) collective-permute-start(bf16[4,128,256]{2,1,0:T(8,128)(2,1)S(1)} %collective-permute-done.8.refs_3_.refs_8_), channel_id=1, source_target_pairs={{0,2},{1,15},{2,4},{3,1},{4,6},{5,3},{6,8},{7,5},{8,10},{9,7},{10,... | collective-permute-start | bytes 786440 | tf_op jit(solution)/shard_map/ppermute | solution.py:54
  44.5 3.2 %shard_map.75 = (f32[2,1024,128]{2,1,0:T(8,128)S(1)}, f32[2,1024,256]{2,1,0:T(8,128)S(1)}) custom-call(s32[2,16]{1,0:T(2,128)S(1)} %get-tuple-element.49.slot_ref, s32[2]{0:T(128)S(1)} %get-tuple-element.47.length_ref, bf16[128,1408]{1,0:T(8,128)(2,1)S(1)} %collective-permute-done.1.refs_0_, bf16[128,1408]{1,0:T(8,128)(2,1)S(1)} %collective-permute-done.2.refs_1_, ...), custom_call_target="tpu_custom_call" | custom-call | flops 1 | bytes 1 | tf_op jit(solution)/shard_map/pallas_call | solution.py:260
  47.7 0.1 collective-permute-done.11.refs_2_.refs_9_
  47.8 3.8 %shard_map.76 = (bf16[128,1024]{1,0:T(8,128)(2,1)}, bf16[128,1024]{1,0:T(8,128)(2,1)}) custom-call(s32[2,16]{1,0:T(2,128)S(1)} %get-tuple-element.49.slot_ref, s32[2]{0:T(128)S(1)} %get-tuple-element.47.length_ref, bf16[128,1408]{1,0:T(8,128)(2,1)S(1)} %collective-permute-done.1.refs_0_, bf16[128,1408]{1,0:T(8,128)(2,1)S(1)} %collective-permute-done.2.refs_1_, ...), custom_call_target="tpu_custom_call" | custom-call | flops 1 | bytes 1 | tf_op jit(solution)/shard_map/pallas_call | solution.py:260
  51.6 2.0 %collective-permute-start.15 = (bf16[128,1024]{1,0:T(8,128)(2,1)}, bf16[128,1024]{1,0:T(8,128)(2,1)S(1)}, u32[]{:S(2)}, u32[]{:S(2)}) collective-permute-start(bf16[128,1024]{1,0:T(8,128)(2,1)} %get-tuple-element.46), channel_id=1, source_target_pairs={{0,16},{1,17},{2,18},{3,19},{4,20},{5,21},{6,22},{7,23},{8,24},{9,... | collective-permute-start | bytes 786440 | tf_op jit(solution)/shard_map/ppermute | solution.py:54
  53.6 4.7 %collective-permute-start.16 = (bf16[128,1024]{1,0:T(8,128)(2,1)}, bf16[128,1024]{1,0:T(8,128)(2,1)S(1)}, u32[]{:S(2)}, u32[]{:S(2)}) collective-permute-start(bf16[128,1024]{1,0:T(8,128)(2,1)} %get-tuple-element.41), channel_id=1, source_target_pairs={{0,17},{1,16},{2,19},{3,18},{4,21},{5,20},{6,23},{7,22},{8,25},{9,... | collective-permute-start | bytes 786440 | tf_op jit(solution)/shard_map/ppermute | solution.py:54
  58.4 0.1 rev.7.length_ref
  58.5 8.8 %shard_map.77 = (bf16[64,1024]{1,0:T(8,128)(2,1)S(1)}, bf16[64,1024]{1,0:T(8,128)(2,1)S(1)}, bf16[128,1024]{1,0:T(8,128)(2,1)S(1)}) custom-call(s32[2,16]{1,0:T(2,128)S(1)} %rev.6.slot_ref, s32[2]{0:T(128)S(1)} %rev.7.length_ref, bf16[128,1408]{1,0:T(8,128)(2,1)S(1)} %collective-permute-done.refs_0_, bf16[128,1408]{1,0:T(8,128)(2,1)S(1)} %copy-done, ...), custom_call_target="tpu_custom_call" | custom-call | flops 1 | bytes 1 | tf_op jit(solution)/shard_map/pallas_call | solution.py:260
  67.2 0.4 collective-permute-start.13
  67.6 0.2 collective-permute-start.14
  67.8 0.8 %collective-permute-done.13.refs_1_ = bf16[64,1024]{1,0:T(8,128)(2,1)S(1)} collective-permute-done((bf16[64,1024]{1,0:T(8,128)(2,1)S(1)}, bf16[64,1024]{1,0:T(8,128)(2,1)S(1)}, u32[]{:S(2)}, u32[]{:S(2)}) %collective-permute-start.13) | collective-permute-done | bytes 131104 | tf_op jit(solution)/shard_map/ppermute | solution.py:54
  68.7 0.3 collective-permute-done.14.refs_2_
  69.0 1.0 %shard_map.78 = bf16[128,4096]{1,0:T(8,128)(2,1)} custom-call(bf16[128,1024]{1,0:T(8,128)(2,1)S(1)} %get-tuple-element.43.refs_0_, bf16[64,1024]{1,0:T(8,128)(2,1)S(1)} %collective-permute-done.13.refs_1_, bf16[64,1024]{1,0:T(8,128)(2,1)S(1)} %collective-permute-done.14.refs_2_, bf16[128,1024]{1,0:T(8,128)(2,1)S(1)} %collective-permute-done.15.refs_3_, ...), custom_call_target="tpu_custom_call" | custom-call | tf_op jit(solution)/shard_map/pallas_call | solution.py:322
  (21 shorter events, 0.3 us)
Async XLA Ops:
  4.1 4.3 %collective-permute-start.3 = (bf16[128,256]{1,0:T(8,128)(2,1)}, bf16[128,256]{1,0:T(8,128)(2,1)S(1)}, u32[]{:S(2)}, u32[]{:S(2)}) collective-permute-start(bf16[128,256]{1,0:T(8,128)(2,1)} %get-tuple-element.31), channel_id=1, source_target_pairs={{0,1},{1,0},{2,3},{3,2},{4,5},{5,4},{6,7},{7,6},{8,9},{9,8},{10,11... | collective-permute-start | bytes 196616 | tf_op jit(solution)/shard_map/ppermute | solution.py:54
  4.9 3.9 %collective-permute-start.4 = (bf16[128,256]{1,0:T(8,128)(2,1)}, bf16[128,256]{1,0:T(8,128)(2,1)S(1)}, u32[]{:S(2)}, u32[]{:S(2)}) collective-permute-start(bf16[128,256]{1,0:T(8,128)(2,1)} %get-tuple-element.32), channel_id=1, source_target_pairs={{0,16},{1,17},{2,18},{3,19},{4,20},{5,21},{6,22},{7,23},{8,24},{9,... | collective-permute-start | bytes 196616 | tf_op jit(solution)/shard_map/ppermute | solution.py:54
  6.1 4.6 %collective-permute-start.5 = (bf16[128,256]{1,0:T(8,128)(2,1)}, bf16[128,256]{1,0:T(8,128)(2,1)S(1)}, u32[]{:S(2)}, u32[]{:S(2)}) collective-permute-start(bf16[128,256]{1,0:T(8,128)(2,1)} %get-tuple-element.33), channel_id=1, source_target_pairs={{0,17},{1,16},{2,19},{3,18},{4,21},{5,20},{6,23},{7,22},{8,25},{9,... | collective-permute-start | bytes 196616 | tf_op jit(solution)/shard_map/ppermute | solution.py:54
  6.6 19.9 %collective-permute-start.1 = (bf16[128,1408]{1,0:T(8,128)(2,1)}, bf16[128,1408]{1,0:T(8,128)(2,1)S(1)}, u32[]{:S(2)}, u32[]{:S(2)}) collective-permute-start(bf16[128,1408]{1,0:T(8,128)(2,1)} %get-tuple-element.28), channel_id=1, source_target_pairs={{0,16},{1,17},{2,18},{3,19},{4,20},{5,21},{6,22},{7,23},{8,24},{9,... | collective-permute-start | bytes 1081352 | tf_op jit(solution)/shard_map/ppermute | solution.py:54
  7.8 18.7 %collective-permute-start.2 = (bf16[128,1408]{1,0:T(8,128)(2,1)}, bf16[128,1408]{1,0:T(8,128)(2,1)S(1)}, u32[]{:S(2)}, u32[]{:S(2)}) collective-permute-start(bf16[128,1408]{1,0:T(8,128)(2,1)} %get-tuple-element.29), channel_id=1, source_target_pairs={{0,17},{1,16},{2,19},{3,18},{4,21},{5,20},{6,23},{7,22},{8,25},{9,... | collective-permute-start | bytes 1081352 | tf_op jit(solution)/shard_map/ppermute | solution.py:54
  8.4 18.2 %collective-permute-start = (bf16[128,1408]{1,0:T(8,128)(2,1)}, bf16[128,1408]{1,0:T(8,128)(2,1)S(1)}, u32[]{:S(2)}, u32[]{:S(2)}) collective-permute-start(bf16[128,1408]{1,0:T(8,128)(2,1)} %get-tuple-element.27), channel_id=1, source_target_pairs={{0,1},{1,0},{2,3},{3,2},{4,5},{5,4},{6,7},{7,6},{8,9},{9,8},{10,11... | collective-permute-start | bytes 1081352 | tf_op jit(solution)/shard_map/ppermute | solution.py:54
  11.6 9.4 %collective-permute-start.9 = (bf16[4,128,256]{2,1,0:T(8,128)(2,1)S(1)}, bf16[4,128,256]{2,1,0:T(8,128)(2,1)S(1)}, u32[]{:S(2)}, u32[]{:S(2)}) collective-permute-start(bf16[4,128,256]{2,1,0:T(8,128)(2,1)S(1)} %pad_maximum_fusion.refs_2_), channel_id=1, source_target_pairs={{0,14},{1,3},{2,0},{3,5},{4,2},{5,7},{6,4},{7,9},{8,6},{9,11},{10,... | collective-permute-start | bytes 786440 | tf_op jit(solution)/shard_map/ppermute | solution.py:54
  13.3 9.8 %collective-permute-start.6 = (bf16[4,128,256]{2,1,0:T(8,128)(2,1)S(1)}, bf16[4,128,256]{2,1,0:T(8,128)(2,1)S(1)}, u32[]{:S(2)}, u32[]{:S(2)}) collective-permute-start(bf16[4,128,256]{2,1,0:T(8,128)(2,1)S(1)} %pad_maximum_fusion.refs_2_), channel_id=1, source_target_pairs={{0,2},{1,15},{2,4},{3,1},{4,6},{5,3},{6,8},{7,5},{8,10},{9,7},{10,... | collective-permute-start | bytes 786440 | tf_op jit(solution)/shard_map/ppermute | solution.py:54
  21.0 14.1 %collective-permute-start.10 = (bf16[4,128,256]{2,1,0:T(8,128)(2,1)S(1)}, bf16[4,128,256]{2,1,0:T(8,128)(2,1)S(1)}, u32[]{:S(2)}, u32[]{:S(2)}) collective-permute-start(bf16[4,128,256]{2,1,0:T(8,128)(2,1)S(1)} %collective-permute-done.9.refs_3_), channel_id=1, source_target_pairs={{0,14},{1,3},{2,0},{3,5},{4,2},{5,7},{6,4},{7,9},{8,6},{9,11},{10,... | collective-permute-start | bytes 786440 | tf_op jit(solution)/shard_map/ppermute | solution.py:54
  23.1 8.3 %collective-permute-start.7 = (bf16[4,128,256]{2,1,0:T(8,128)(2,1)S(1)}, bf16[4,128,256]{2,1,0:T(8,128)(2,1)S(1)}, u32[]{:S(2)}, u32[]{:S(2)}) collective-permute-start(bf16[4,128,256]{2,1,0:T(8,128)(2,1)S(1)} %collective-permute-done.6.refs_4_), channel_id=1, source_target_pairs={{0,2},{1,15},{2,4},{3,1},{4,6},{5,3},{6,8},{7,5},{8,10},{9,7},{10,... | collective-permute-start | bytes 786440 | tf_op jit(solution)/shard_map/ppermute | solution.py:54
  31.5 9.3 %collective-permute-start.8 = (bf16[4,128,256]{2,1,0:T(8,128)(2,1)S(1)}, bf16[4,128,256]{2,1,0:T(8,128)(2,1)S(1)}, u32[]{:S(2)}, u32[]{:S(2)}) collective-permute-start(bf16[4,128,256]{2,1,0:T(8,128)(2,1)S(1)} %collective-permute-done.7.refs_6_), channel_id=1, source_target_pairs={{0,2},{1,15},{2,4},{3,1},{4,6},{5,3},{6,8},{7,5},{8,10},{9,7},{10,... | collective-permute-start | bytes 786440 | tf_op jit(solution)/shard_map/ppermute | solution.py:54
  35.1 9.4 %collective-permute-start.12 = (bf16[4,128,256]{2,1,0:T(8,128)(2,1)S(1)}, bf16[4,128,256]{2,1,0:T(8,128)(2,1)S(1)}, u32[]{:S(2)}, u32[]{:S(2)}) collective-permute-start(bf16[4,128,256]{2,1,0:T(8,128)(2,1)S(1)} %collective-permute-done.10.refs_5_), channel_id=1, source_target_pairs={{0,14},{1,3},{2,0},{3,5},{4,2},{5,7},{6,4},{7,9},{8,6},{9,11},{10,... | collective-permute-start | bytes 786440 | tf_op jit(solution)/shard_map/ppermute | solution.py:54
  40.8 7.0 %collective-permute-start.11 = (bf16[4,128,256]{2,1,0:T(8,128)(2,1)S(1)}, bf16[4,128,256]{2,1,0:T(8,128)(2,1)S(1)}, u32[]{:S(2)}, u32[]{:S(2)}) collective-permute-start(bf16[4,128,256]{2,1,0:T(8,128)(2,1)S(1)} %collective-permute-done.8.refs_3_.refs_8_), channel_id=1, source_target_pairs={{0,2},{1,15},{2,4},{3,1},{4,6},{5,3},{6,8},{7,5},{8,10},{9,7},{10,... | collective-permute-start | bytes 786440 | tf_op jit(solution)/shard_map/ppermute | solution.py:54
  47.7 10.8 %copy-start = (bf16[128,1408]{1,0:T(8,128)(2,1)S(1)}, bf16[128,1408]{1,0:T(8,128)(2,1)}, u32[]{:S(2)}) copy-start(bf16[128,1408]{1,0:T(8,128)(2,1)} %get-tuple-element.26.refs_1_) | copy-start | bytes 1081348
  51.6 17.3 %collective-permute-start.15 = (bf16[128,1024]{1,0:T(8,128)(2,1)}, bf16[128,1024]{1,0:T(8,128)(2,1)S(1)}, u32[]{:S(2)}, u32[]{:S(2)}) collective-permute-start(bf16[128,1024]{1,0:T(8,128)(2,1)} %get-tuple-element.46), channel_id=1, source_target_pairs={{0,16},{1,17},{2,18},{3,19},{4,20},{5,21},{6,22},{7,23},{8,24},{9,... | collective-permute-start | bytes 786440 | tf_op jit(solution)/shard_map/ppermute | solution.py:54
  53.6 15.3 %collective-permute-start.16 = (bf16[128,1024]{1,0:T(8,128)(2,1)}, bf16[128,1024]{1,0:T(8,128)(2,1)S(1)}, u32[]{:S(2)}, u32[]{:S(2)}) collective-permute-start(bf16[128,1024]{1,0:T(8,128)(2,1)} %get-tuple-element.41), channel_id=1, source_target_pairs={{0,17},{1,16},{2,19},{3,18},{4,21},{5,20},{6,23},{7,22},{8,25},{9,... | collective-permute-start | bytes 786440 | tf_op jit(solution)/shard_map/ppermute | solution.py:54
  67.2 1.4 %collective-permute-start.13 = (bf16[64,1024]{1,0:T(8,128)(2,1)S(1)}, bf16[64,1024]{1,0:T(8,128)(2,1)S(1)}, u32[]{:S(2)}, u32[]{:S(2)}) collective-permute-start(bf16[64,1024]{1,0:T(8,128)(2,1)S(1)} %get-tuple-element.44), channel_id=1, source_target_pairs={{0,1},{1,0},{2,3},{3,2},{4,5},{5,4},{6,7},{7,6},{8,9},{9,8},{10,11... | collective-permute-start | bytes 393224 | tf_op jit(solution)/shard_map/ppermute | solution.py:54
  67.6 1.3 %collective-permute-start.14 = (bf16[64,1024]{1,0:T(8,128)(2,1)S(1)}, bf16[64,1024]{1,0:T(8,128)(2,1)S(1)}, u32[]{:S(2)}, u32[]{:S(2)}) collective-permute-start(bf16[64,1024]{1,0:T(8,128)(2,1)S(1)} %get-tuple-element.45), channel_id=1, source_target_pairs={{0,1},{1,0},{2,3},{3,2},{4,5},{5,4},{6,7},{7,6},{8,9},{9,8},{10,11... | collective-permute-start | bytes 393224 | tf_op jit(solution)/shard_map/ppermute | solution.py:54

commit v2 on v1

--- a/solution.py
+++ b/solution.py
@@ -21,6 +21,7 @@
 PLANE = 4
 DEPTH = 8
 WAVE = 5
+NEAR = 3
 SCALE = DH**-0.5 * math.log2(math.e)
 
 
@@ -64,32 +65,43 @@
     return [2 * x + c, 2 * x + 1 - c, 2 * (1 - x) + c, 2 * (1 - x) + 1 - c]
 
 
-def pack(table_ref, length_ref, pk_ref, pv_ref, q_ref, k_ref, v_ref, *refs):
-    pool, request, sems = refs[:PLANE], refs[PLANE : 2 * PLANE], refs[2 * PLANE]
-    copies = []
-
+def mover(copies, sems):
     def move(source, target):
         copies.append(pltpu.make_async_copy(source, target, sems.at[len(copies)]))
         copies[-1].start()
 
+    return move
+
+
+def pack_pool(k_ref, v_ref, *refs):
+    outs, copies = refs[:PLANE], []
+    move = mover(copies, refs[PLANE])
     heads = peer_heads()
-    for j in range(PLANE):
+    for j in (1, 2, 3, 0):
         own = column(heads[j], DH)
-        move(pk_ref.at[:, own], pool[j].at[:, :DH])
-        move(pv_ref.at[:, own], pool[j].at[:, DH:])
-    for j in range(PLANE):
+        move(k_ref.at[:, own], outs[j].at[:, :DH])
+        move(v_ref.at[:, own], outs[j].at[:, DH:])
+    for copy in copies:
+        copy.wait()
+
+
+def pack_request(table_ref, length_ref, q_ref, k_ref, v_ref, *refs):
+    outs, copies = refs[:PLANE], []
+    move = mover(copies, refs[PLANE])
+    heads = peer_heads()
+    for j in (2, 3, 1, 0):
         own = column(heads[j], DH)
-        move(q_ref.at[:, column(heads[j], GW)], request[j].at[:, :GW])
-        move(k_ref.at[:, own], request[j].at[:, GW : GW + DH])
-        move(v_ref.at[:, own], request[j].at[:, GW + DH : GW + 2 * DH])
+        move(q_ref.at[:, column(heads[j], GW)], outs[j].at[:, :GW])
+        move(k_ref.at[:, own], outs[j].at[:, GW : GW + DH])
+        move(v_ref.at[:, own], outs[j].at[:, GW + DH : GW + 2 * DH])
     lane = lax.broadcasted_iota(jnp.int32, (16, DH), 1)
     meta = jnp.where(lane == MAXB, length_ref[0], 0)
     for i in range(MAXB):
         meta = jnp.where(lane == i, table_ref[0, i], meta)
     meta = meta.astype(jnp.float32).astype(jnp.bfloat16)
     for j in range(PLANE):
-        request[j][:16, GW + 2 * DH :] = meta
-        request[j][16:, GW + 2 * DH :] = jnp.zeros((BS - 16, DH), jnp.bfloat16)
+        outs[j][:16, GW + 2 * DH :] = meta
+        outs[j][16:, GW + 2 * DH :] = jnp.zeros((BS - 16, DH), jnp.bfloat16)
     for copy in copies:
         copy.wait()
 
@@ -278,40 +290,54 @@
 
 
 def body(queries, new_keys, new_values, prefix_keys, prefix_values, block_table, prefix_blocks):
+    pool = pl.pallas_call(
+        pack_pool,
+        out_shape=[jax.ShapeDtypeStruct((BS, 2 * DH), jnp.bfloat16)] * PLANE,
+        in_specs=[HBM] * 2,
+        out_specs=[VMEM] * PLANE,
+        scratch_shapes=[pltpu.SemaphoreType.DMA((2 * PLANE,))],
+    )(prefix_keys, prefix_values)
+    ahead, _ = lax.optimization_barrier((queries, pool))
+    request = pl.pallas_call(
+        pack_request,
+        out_shape=[jax.ShapeDtypeStruct((BS, MSG), jnp.bfloat16)] * PLANE,
+        in_specs=[SMEM] * 2 + [HBM] * 3,
+        out_specs=[VMEM] * PLANE,
+        scratch_shapes=[pltpu.SemaphoreType.DMA((3 * PLANE,))],
+        cost_estimate=pl.CostEstimate(flops=1, bytes_accessed=1, transcendentals=1),
+    )(block_table, prefix_blocks, ahead, new_keys, new_values)
+    arrived = [pool[0]] + [send(o, t) for o, t in zip(pool[1:], PEERS)]
+    arrived, request = lax.optimization_barrier((arrived, request))
+    piece = jnp.stack(arrived)
+    msgs = [request[0]] + [send(o, t) for o, t in zip(request[1:], PEERS)]
+
     me = lax.axis_index("blk")
     x, z, c = me // 16, (me // 2) % 8, me % 2
-    shards = [jax.ShapeDtypeStruct((BS, w), jnp.bfloat16) for w in (2 * DH, MSG) for _ in range(PLANE)]
-    packed = pl.pallas_call(
-        pack,
-        out_shape=shards,
-        in_specs=[SMEM] * 2 + [HBM] * 5,
-        out_specs=[VMEM] * len(shards),
-        scratch_shapes=[pltpu.SemaphoreType.DMA((5 * PLANE,))],
-    )(block_table, prefix_blocks, prefix_keys, prefix_values, queries, new_keys, new_values)
-    pool, request = packed[:PLANE], packed[PLANE:]
-    arrived = [pool[0]] + [send(o, t) for o, t in zip(pool[1:], PEERS)]
-    piece = jnp.stack(arrived)
-    msgs = [request[0]] + [send(o, t) for o, t in zip(request[1:], PEERS)]
-
+
+    def entries(chosen):
+        info = jnp.stack([m[0, GW + 2 * DH : GW + 2 * DH + MAXB + 1] for m in chosen]).astype(jnp.int32)
+        table, lengths = info[:, :MAXB], info[:, MAXB]
+        deep = (((table // 2) % 8 - z) * (1 - 2 * c)) % 8
+        order = jnp.where(deep < 4, jnp.maximum(2 * deep - 1, 0), jnp.minimum(2 * (8 - deep), 7))
+        return order * 4 + (table // 16 ^ x) * 2 + (table % 2 ^ c), lengths
+
+    near, far = msgs[1::-1], msgs[2:]
+    near_work, far_work = entries(near), entries(far)
     a, b = [piece], [piece]
-    for _ in range(3):
+    for _ in range(2):
         a.append(send(a[-1], AHEAD))
         b.append(send(b[-1], BACK))
-    planes = [a[0], b[1], a[1], b[2], a[2], b[3], a[3]]
-
-    info = jnp.stack([m[0, GW + 2 * DH : GW + 2 * DH + MAXB + 1] for m in msgs]).astype(jnp.int32)
-    table, lengths = info[:, :MAXB], info[:, MAXB]
-    deep = (((table // 2) % 8 - z) * (1 - 2 * c)) % 8
-    order = jnp.where(deep < 4, jnp.maximum(2 * deep - 1, 0), jnp.minimum(2 * (8 - deep), 7))
-    slots = order * 4 + (table // 16 ^ x) * 2 + (table % 2 ^ c)
-
-    state = run_attend(slots[2:], lengths[2:], msgs[2:], planes, 0, WAVE)
-    last, state = lax.optimization_barrier((a[3], state))
+    planes = [a[0], b[1], a[1], b[2], a[2]]
+    near_state = run_attend(*near_work, near, planes, 0, NEAR)
+    last, near_state = lax.optimization_barrier(((a[2], b[2]), near_state))
+    planes += [send(last[1], BACK), send(last[0], AHEAD)]
+    state = run_attend(*far_work, far, planes, 0, WAVE)
+    last, state = lax.optimization_barrier((planes[-1], state))
     planes.append(send(last, AHEAD))
-    state = run_attend(slots[2:], lengths[2:], msgs[2:], planes, WAVE, DEPTH - 1, state)
-    across, diagonal = run_attend(slots[2:], lengths[2:], msgs[2:], planes, DEPTH - 1, DEPTH, state, (1, 1))
-    late, _ = lax.optimization_barrier((msgs[1], diagonal))
-    *sibling, mine = run_attend(slots[1::-1], lengths[1::-1], [late, msgs[0]], planes, 0, DEPTH, (), (2, 1))
+    state = run_attend(*far_work, far, planes, WAVE, DEPTH - 1, state)
+    across, diagonal = run_attend(*far_work, far, planes, DEPTH - 1, DEPTH, state, (1, 1))
+    near_state, _ = lax.optimization_barrier((near_state, diagonal))
+    *sibling, mine = run_attend(*near_work, near, planes, NEAR, DEPTH, near_state, (2, 1))
     parts = [
         [mine],
         [send(p, SIBLING) for p in sibling],

time: 70.8 us -> 67.4 us (0.952)
  the two profiles are of different devices: /device:TPU:9 before, /device:TPU:1 now
where the time goes in v2:
time: 67.4 us; the launch traced here: 67.2 us
  starting transfers between devices  26.1 us (39%)
  Pallas kernels  25.6 us (38%)
  waiting for transfers between devices  11.5 us (17%)
  local copies, waits for them, and re-layouts  2.04 us (3%)
  between operations  0.98 us (1%)
  other arithmetic  0.97 us (1%)
    ppermute x17, starting transfers between devices, send(): return lax.ppermute(piece, 'blk', table)  26.1 us
    pallas_call x5, Pallas kernels, run_attend(): pl.pallas_call(functools.partial(attend, low, high, not state, cuts), out...  19.7 us
    ppermute x17, waiting for transfers between devices, send(): return lax.ppermute(piece, 'blk', table)  11.5 us
    pallas_call x1, Pallas kernels, body(): pl.pallas_call(pack_request, out_shape=[jax.ShapeDtypeStruct((BS, MSG), j...  3.18 us
    pallas_call x1, Pallas kernels, body(): pl.pallas_call(pack_pool, out_shape=[jax.ShapeDtypeStruct((BS, 2 * DH), j...  1.65 us
  transfers between devices with their start and end apart: 17, of which 8 were waited for; matrix products, arithmetic and copies ran while one was open for 3% of the time, Pallas kernels for 31%

profile of v2, /device:TPU:1, one launch (start us, length us, event | category | flops | bytes accessed | tf_op | source)
XLA Modules:
  0.0 67.2 jit_solution(1772336248707340704)
XLA Ops:
  0.0 1.7 %shard_map.73 = (bf16[128,256]{1,0:T(8,128)(2,1)}, bf16[128,256]{1,0:T(8,128)(2,1)}, bf16[128,256]{1,0:T(8,128)(2,1)}, bf16[128,256]{1,0:T(8,128)(2,1)}) custom-call(bf16[128,512]{1,0:T(8,128)(2,1)} %k_ref.2, bf16[128,512]{1,0:T(8,128)(2,1)} %v_ref.2), custom_call_target="tpu_custom_call" | custom-call | tf_op jit(solution)/shard_map/pallas_call | solution.py:293
  1.7 3.3 %collective-permute-start = (bf16[128,256]{1,0:T(8,128)(2,1)}, bf16[128,256]{1,0:T(8,128)(2,1)S(1)}, u32[]{:S(2)}, u32[]{:S(2)}) collective-permute-start(bf16[128,256]{1,0:T(8,128)(2,1)} %get-tuple-element.43), channel_id=1, source_target_pairs={{0,1},{1,0},{2,3},{3,2},{4,5},{5,4},{6,7},{7,6},{8,9},{9,8},{10,11... | collective-permute-start | bytes 196616 | tf_op jit(solution)/shard_map/ppermute | solution.py:55
  5.0 1.7 %collective-permute-start.2 = (bf16[128,256]{1,0:T(8,128)(2,1)}, bf16[128,256]{1,0:T(8,128)(2,1)S(1)}, u32[]{:S(2)}, u32[]{:S(2)}) collective-permute-start(bf16[128,256]{1,0:T(8,128)(2,1)} %get-tuple-element.45), channel_id=1, source_target_pairs={{0,17},{1,16},{2,19},{3,18},{4,21},{5,20},{6,23},{7,22},{8,25},{9,... | collective-permute-start | bytes 196616 | tf_op jit(solution)/shard_map/ppermute | solution.py:55
  7.4 3.2 %shard_map.74 = (bf16[128,1408]{1,0:T(8,128)(2,1)}, bf16[128,1408]{1,0:T(8,128)(2,1)}, bf16[128,1408]{1,0:T(8,128)(2,1)}, bf16[128,1408]{1,0:T(8,128)(2,1)}) custom-call(s32[1,16]{1,0:T(1,128)} %table_ref.1, s32[1]{0:T(128)S(6)} %copy.8.length_ref, bf16[128,4096]{1,0:T(8,128)(2,1)} %q_ref, bf16[128,512]{1,0:T(8,128)(2,1)} %k_ref.3, bf16[128,512]{1,0:T(8,128)(2,1)} %v_ref.3), custom_call_target="tpu_custom_call" | custom-call | flops 1 | bytes 1 | tf_op jit(solution)/shard_map/pallas_call | solution.py:301
  10.6 0.2 collective-permute-start.3
  10.8 0.9 %pad_maximum_fusion.refs_2_ = bf16[4,128,256]{2,1,0:T(8,128)(2,1)S(1)} fusion(bf16[1,128,256]{2,1,0:T(8,128)(2,1)S(1)} %bitcast.7, bf16[1,128,256]{2,1,0:T(8,128)(2,1)S(1)} %bitcast.6, bf16[1,128,256]{2,1,0:T(8,128)(2,1)S(1)} %bitcast.5, bf16[1,128,256]{2,1,0:T(8,128)(2,1)} %bitcast.4), kind=kLoop, calls=%fused_computation | loop fusion | flops 393216 | bytes 524288 | tf_op jit(solution)/shard_map/stack | solution.py:311
  11.8 3.9 %collective-permute-start.6 = (bf16[4,128,256]{2,1,0:T(8,128)(2,1)S(1)}, bf16[4,128,256]{2,1,0:T(8,128)(2,1)S(1)}, u32[]{:S(2)}, u32[]{:S(2)}) collective-permute-start(bf16[4,128,256]{2,1,0:T(8,128)(2,1)S(1)} %pad_maximum_fusion.refs_2_), channel_id=1, source_target_pairs={{0,2},{1,15},{2,4},{3,1},{4,6},{5,3},{6,8},{7,5},{8,10},{9,7},{10,... | collective-permute-start | bytes 786440 | tf_op jit(solution)/shard_map/ppermute | solution.py:55
  15.7 1.2 %collective-permute-start.10 = (bf16[128,1408]{1,0:T(8,128)(2,1)}, bf16[128,1408]{1,0:T(8,128)(2,1)S(1)}, u32[]{:S(2)}, u32[]{:S(2)}) collective-permute-start(bf16[128,1408]{1,0:T(8,128)(2,1)} %get-tuple-element.61), channel_id=1, source_target_pairs={{0,16},{1,17},{2,18},{3,19},{4,20},{5,21},{6,22},{7,23},{8,24},{9,... | collective-permute-start | bytes 1081352 | tf_op jit(solution)/shard_map/ppermute | solution.py:55
  16.9 1.0 %collective-permute-start.11 = (bf16[128,1408]{1,0:T(8,128)(2,1)}, bf16[128,1408]{1,0:T(8,128)(2,1)S(1)}, u32[]{:S(2)}, u32[]{:S(2)}) collective-permute-start(bf16[128,1408]{1,0:T(8,128)(2,1)} %get-tuple-element.62), channel_id=1, source_target_pairs={{0,17},{1,16},{2,19},{3,18},{4,21},{5,20},{6,23},{7,22},{8,25},{9,... | collective-permute-start | bytes 1081352 | tf_op jit(solution)/shard_map/ppermute | solution.py:55
  17.9 0.7 %slice.25 = bf16[1,17]{1,0:T(2,128)(2,1)S(1)} slice(bf16[128,1408]{1,0:T(8,128)(2,1)} %get-tuple-element.52.refs_1_), slice={[0:1], [1280:1297]} | slice | bytes 68 | tf_op jit(solution)/shard_map/slice | solution.py:318
  18.6 0.8 %collective-permute-done.4.refs_3_ = bf16[4,128,256]{2,1,0:T(8,128)(2,1)S(1)} collective-permute-done((bf16[4,128,256]{2,1,0:T(8,128)(2,1)S(1)}, bf16[4,128,256]{2,1,0:T(8,128)(2,1)S(1)}, u32[]{:S(2)}, u32[]{:S(2)}) %collective-permute-start.4) | collective-permute-done | bytes 262176 | tf_op jit(solution)/shard_map/ppermute | solution.py:55
  19.4 1.8 %collective-permute-done.6.refs_4_ = bf16[4,128,256]{2,1,0:T(8,128)(2,1)S(1)} collective-permute-done((bf16[4,128,256]{2,1,0:T(8,128)(2,1)S(1)}, bf16[4,128,256]{2,1,0:T(8,128)(2,1)S(1)}, u32[]{:S(2)}, u32[]{:S(2)}) %collective-permute-start.6) | collective-permute-done | bytes 262176 | tf_op jit(solution)/shard_map/ppermute | solution.py:55
  21.2 3.4 %collective-permute-start.7 = (bf16[4,128,256]{2,1,0:T(8,128)(2,1)S(1)}, bf16[4,128,256]{2,1,0:T(8,128)(2,1)S(1)}, u32[]{:S(2)}, u32[]{:S(2)}) collective-permute-start(bf16[4,128,256]{2,1,0:T(8,128)(2,1)S(1)} %collective-permute-done.6.refs_4_), channel_id=1, source_target_pairs={{0,2},{1,15},{2,4},{3,1},{4,6},{5,3},{6,8},{7,5},{8,10},{9,7},{10,... | collective-permute-start | bytes 786440 | tf_op jit(solution)/shard_map/ppermute | solution.py:55
  24.9 1.0 %copy-done = bf16[128,1408]{1,0:T(8,128)(2,1)S(1)} copy-done((bf16[128,1408]{1,0:T(8,128)(2,1)S(1)}, bf16[128,1408]{1,0:T(8,128)(2,1)}, u32[]{:S(2)}) %copy-start) | copy-done | bytes 360472
  25.8 5.3 %shard_map.75 = (f32[2,1024,128]{2,1,0:T(8,128)S(1)}, f32[2,1024,256]{2,1,0:T(8,128)S(1)}) custom-call(s32[2,16]{1,0:T(2,128)S(1)} %fusion.4.slot_ref, s32[2]{0:T(128)S(1)} %slice_reduce_fusion.1.length_ref, bf16[128,1408]{1,0:T(8,128)(2,1)S(1)} %collective-permute-done.3.refs_0_, bf16[128,1408]{1,0:T(8,128)(2,1)S(1)} %copy-done, ...), custom_call_target="tpu_custom_call" | custom-call | flops 1 | bytes 1 | tf_op jit(solution)/shard_map/pallas_call | solution.py:272
  31.2 2.6 %collective-permute-done.11.refs_1_ = bf16[128,1408]{1,0:T(8,128)(2,1)S(1)} collective-permute-done((bf16[128,1408]{1,0:T(8,128)(2,1)}, bf16[128,1408]{1,0:T(8,128)(2,1)S(1)}, u32[]{:S(2)}, u32[]{:S(2)}) %collective-permute-start.11) | collective-permute-done | bytes 360480 | tf_op jit(solution)/shard_map/ppermute | solution.py:55
  33.8 1.5 %collective-permute-start.9 = (bf16[4,128,256]{2,1,0:T(8,128)(2,1)S(1)}, bf16[4,128,256]{2,1,0:T(8,128)(2,1)S(1)}, u32[]{:S(2)}, u32[]{:S(2)}) collective-permute-start(bf16[4,128,256]{2,1,0:T(8,128)(2,1)S(1)} %collective-permute-done.7.refs_6_.refs_3_), channel_id=1, source_target_pairs={{0,2},{1,15},{2,4},{3,1},{4,6},{5,3},{6,8},{7,5},{8,10},{9,7},{10,... | collective-permute-start | bytes 786440 | tf_op jit(solution)/shard_map/ppermute | solution.py:55
  35.3 0.2 slice_reduce_fusion.length_ref
  35.7 3.8 %shard_map.76 = (f32[2,1024,128]{2,1,0:T(8,128)S(1)}, f32[2,1024,256]{2,1,0:T(8,128)S(1)}) custom-call(s32[2,16]{1,0:T(2,128)S(1)} %fusion.10.slot_ref, s32[2]{0:T(128)S(1)} %slice_reduce_fusion.length_ref, bf16[128,1408]{1,0:T(8,128)(2,1)S(1)} %collective-permute-done.10.refs_0_, bf16[128,1408]{1,0:T(8,128)(2,1)S(1)} %collective-permute-done.11.refs_1_, ...), custom_call_target="tpu_custom_call" | custom-call | flops 1 | bytes 1 | tf_op jit(solution)/shard_map/pallas_call | solution.py:272
  39.5 2.3 %collective-permute-done.9.refs_3_.refs_5_ = bf16[4,128,256]{2,1,0:T(8,128)(2,1)S(1)} collective-permute-done((bf16[4,128,256]{2,1,0:T(8,128)(2,1)S(1)}, bf16[4,128,256]{2,1,0:T(8,128)(2,1)S(1)}, u32[]{:S(2)}, u32[]{:S(2)}) %collective-permute-start.9) | collective-permute-done | bytes 262176 | tf_op jit(solution)/shard_map/ppermute | solution.py:55
  41.8 3.0 %collective-permute-start.12 = (bf16[4,128,256]{2,1,0:T(8,128)(2,1)S(1)}, bf16[4,128,256]{2,1,0:T(8,128)(2,1)S(1)}, u32[]{:S(2)}, u32[]{:S(2)}) collective-permute-start(bf16[4,128,256]{2,1,0:T(8,128)(2,1)S(1)} %collective-permute-done.9.refs_3_.refs_5_), channel_id=1, source_target_pairs={{0,2},{1,15},{2,4},{3,1},{4,6},{5,3},{6,8},{7,5},{8,10},{9,7},{10,... | collective-permute-start | bytes 786440 | tf_op jit(solution)/shard_map/ppermute | solution.py:55
  44.8 3.1 %shard_map.77 = (f32[2,1024,128]{2,1,0:T(8,128)S(1)}, f32[2,1024,256]{2,1,0:T(8,128)S(1)}) custom-call(s32[2,16]{1,0:T(2,128)S(1)} %fusion.10.slot_ref, s32[2]{0:T(128)S(1)} %slice_reduce_fusion.length_ref, bf16[128,1408]{1,0:T(8,128)(2,1)S(1)} %collective-permute-done.10.refs_0_, bf16[128,1408]{1,0:T(8,128)(2,1)S(1)} %collective-permute-done.11.refs_1_, ...), custom_call_target="tpu_custom_call" | custom-call | flops 1 | bytes 1 | tf_op jit(solution)/shard_map/pallas_call | solution.py:272
  48.2 2.3 %shard_map.78 = (bf16[128,1024]{1,0:T(8,128)(2,1)S(1)}, bf16[128,1024]{1,0:T(8,128)(2,1)S(1)}) custom-call(s32[2,16]{1,0:T(2,128)S(1)} %fusion.10.slot_ref, s32[2]{0:T(128)S(1)} %slice_reduce_fusion.length_ref, bf16[128,1408]{1,0:T(8,128)(2,1)S(1)} %collective-permute-done.10.refs_0_, bf16[128,1408]{1,0:T(8,128)(2,1)S(1)} %collective-permute-done.11.refs_1_, ...), custom_call_target="tpu_custom_call" | custom-call | flops 1 | bytes 1 | tf_op jit(solution)/shard_map/pallas_call | solution.py:272
  50.5 2.2 %collective-permute-start.15 = (bf16[128,1024]{1,0:T(8,128)(2,1)S(1)}, bf16[128,1024]{1,0:T(8,128)(2,1)S(1)}, u32[]{:S(2)}, u32[]{:S(2)}) collective-permute-start(bf16[128,1024]{1,0:T(8,128)(2,1)S(1)} %get-tuple-element.78), channel_id=1, source_target_pairs={{0,16},{1,17},{2,18},{3,19},{4,20},{5,21},{6,22},{7,23},{8,24},{9,... | collective-permute-start | bytes 786440 | tf_op jit(solution)/shard_map/ppermute | solution.py:55
  52.6 3.8 %collective-permute-start.16 = (bf16[128,1024]{1,0:T(8,128)(2,1)S(1)}, bf16[128,1024]{1,0:T(8,128)(2,1)S(1)}, u32[]{:S(2)}, u32[]{:S(2)}) collective-permute-start(bf16[128,1024]{1,0:T(8,128)(2,1)S(1)} %get-tuple-element.72), channel_id=1, source_target_pairs={{0,17},{1,16},{2,19},{3,18},{4,21},{5,20},{6,23},{7,22},{8,25},{9,... | collective-permute-start | bytes 786440 | tf_op jit(solution)/shard_map/ppermute | solution.py:55
  56.4 5.1 %shard_map.79 = (bf16[64,1024]{1,0:T(8,128)(2,1)S(1)}, bf16[64,1024]{1,0:T(8,128)(2,1)S(1)}, bf16[128,1024]{1,0:T(8,128)(2,1)S(1)}) custom-call(s32[2,16]{1,0:T(2,128)S(1)} %fusion.4.slot_ref, s32[2]{0:T(128)S(1)} %slice_reduce_fusion.1.length_ref, bf16[128,1408]{1,0:T(8,128)(2,1)S(1)} %collective-permute-done.3.refs_0_, bf16[128,1408]{1,0:T(8,128)(2,1)S(1)} %copy-done.1, ...), custom_call_target="tpu_custom_call" | custom-call | flops 1 | bytes 1 | tf_op jit(solution)/shard_map/pallas_call | solution.py:272
  61.6 0.4 collective-permute-start.13
  62.0 0.2 collective-permute-start.14
  62.2 0.8 %collective-permute-done.13.refs_1_ = bf16[64,1024]{1,0:T(8,128)(2,1)S(1)} collective-permute-done((bf16[64,1024]{1,0:T(8,128)(2,1)S(1)}, bf16[64,1024]{1,0:T(8,128)(2,1)S(1)}, u32[]{:S(2)}, u32[]{:S(2)}) %collective-permute-start.13) | collective-permute-done | bytes 131104 | tf_op jit(solution)/shard_map/ppermute | solution.py:55
  63.0 0.3 collective-permute-done.14.refs_2_
  63.3 2.7 %collective-permute-done.16.refs_4_ = bf16[128,1024]{1,0:T(8,128)(2,1)S(1)} collective-permute-done((bf16[128,1024]{1,0:T(8,128)(2,1)S(1)}, bf16[128,1024]{1,0:T(8,128)(2,1)S(1)}, u32[]{:S(2)}, u32[]{:S(2)}) %collective-permute-start.16) | collective-permute-done | bytes 262176 | tf_op jit(solution)/shard_map/ppermute | solution.py:55
  66.0 1.0 %shard_map.80 = bf16[128,4096]{1,0:T(8,128)(2,1)} custom-call(bf16[128,1024]{1,0:T(8,128)(2,1)S(1)} %get-tuple-element.75.refs_0_, bf16[64,1024]{1,0:T(8,128)(2,1)S(1)} %collective-permute-done.13.refs_1_, bf16[64,1024]{1,0:T(8,128)(2,1)S(1)} %collective-permute-done.14.refs_2_, bf16[128,1024]{1,0:T(8,128)(2,1)S(1)} %collective-permute-done.15.refs_3_, ...), custom_call_target="tpu_custom_call" | custom-call | tf_op jit(solution)/shard_map/pallas_call | solution.py:348
  (25 shorter events, 0.8 us)
Async XLA Ops:
  1.7 8.9 %collective-permute-start = (bf16[128,256]{1,0:T(8,128)(2,1)}, bf16[128,256]{1,0:T(8,128)(2,1)S(1)}, u32[]{:S(2)}, u32[]{:S(2)}) collective-permute-start(bf16[128,256]{1,0:T(8,128)(2,1)} %get-tuple-element.43), channel_id=1, source_target_pairs={{0,1},{1,0},{2,3},{3,2},{4,5},{5,4},{6,7},{7,6},{8,9},{9,8},{10,11... | collective-permute-start | bytes 196616 | tf_op jit(solution)/shard_map/ppermute | solution.py:55
  5.0 5.6 %collective-permute-start.1 = (bf16[128,256]{1,0:T(8,128)(2,1)}, bf16[128,256]{1,0:T(8,128)(2,1)S(1)}, u32[]{:S(2)}, u32[]{:S(2)}) collective-permute-start(bf16[128,256]{1,0:T(8,128)(2,1)} %get-tuple-element.44), channel_id=1, source_target_pairs={{0,16},{1,17},{2,18},{3,19},{4,20},{5,21},{6,22},{7,23},{8,24},{9,... | collective-permute-start | bytes 196616 | tf_op jit(solution)/shard_map/ppermute | solution.py:55
  5.0 5.6 %collective-permute-start.2 = (bf16[128,256]{1,0:T(8,128)(2,1)}, bf16[128,256]{1,0:T(8,128)(2,1)S(1)}, u32[]{:S(2)}, u32[]{:S(2)}) collective-permute-start(bf16[128,256]{1,0:T(8,128)(2,1)} %get-tuple-element.45), channel_id=1, source_target_pairs={{0,17},{1,16},{2,19},{3,18},{4,21},{5,20},{6,23},{7,22},{8,25},{9,... | collective-permute-start | bytes 196616 | tf_op jit(solution)/shard_map/ppermute | solution.py:55
  10.6 14.0 %collective-permute-start.3 = (bf16[128,1408]{1,0:T(8,128)(2,1)}, bf16[128,1408]{1,0:T(8,128)(2,1)S(1)}, u32[]{:S(2)}, u32[]{:S(2)}) collective-permute-start(bf16[128,1408]{1,0:T(8,128)(2,1)} %get-tuple-element.51), channel_id=1, source_target_pairs={{0,1},{1,0},{2,3},{3,2},{4,5},{5,4},{6,7},{7,6},{8,9},{9,8},{10,11... | collective-permute-start | bytes 1081352 | tf_op jit(solution)/shard_map/ppermute | solution.py:55
  11.7 7.7 %collective-permute-start.4 = (bf16[4,128,256]{2,1,0:T(8,128)(2,1)S(1)}, bf16[4,128,256]{2,1,0:T(8,128)(2,1)S(1)}, u32[]{:S(2)}, u32[]{:S(2)}) collective-permute-start(bf16[4,128,256]{2,1,0:T(8,128)(2,1)S(1)} %pad_maximum_fusion.refs_2_), channel_id=1, source_target_pairs={{0,14},{1,3},{2,0},{3,5},{4,2},{5,7},{6,4},{7,9},{8,6},{9,11},{10,... | collective-permute-start | bytes 786440 | tf_op jit(solution)/shard_map/ppermute | solution.py:55
  11.8 9.4 %collective-permute-start.6 = (bf16[4,128,256]{2,1,0:T(8,128)(2,1)S(1)}, bf16[4,128,256]{2,1,0:T(8,128)(2,1)S(1)}, u32[]{:S(2)}, u32[]{:S(2)}) collective-permute-start(bf16[4,128,256]{2,1,0:T(8,128)(2,1)S(1)} %pad_maximum_fusion.refs_2_), channel_id=1, source_target_pairs={{0,2},{1,15},{2,4},{3,1},{4,6},{5,3},{6,8},{7,5},{8,10},{9,7},{10,... | collective-permute-start | bytes 786440 | tf_op jit(solution)/shard_map/ppermute | solution.py:55
  15.7 15.5 %collective-permute-start.10 = (bf16[128,1408]{1,0:T(8,128)(2,1)}, bf16[128,1408]{1,0:T(8,128)(2,1)S(1)}, u32[]{:S(2)}, u32[]{:S(2)}) collective-permute-start(bf16[128,1408]{1,0:T(8,128)(2,1)} %get-tuple-element.61), channel_id=1, source_target_pairs={{0,16},{1,17},{2,18},{3,19},{4,20},{5,21},{6,22},{7,23},{8,24},{9,... | collective-permute-start | bytes 1081352 | tf_op jit(solution)/shard_map/ppermute | solution.py:55
  16.9 16.9 %collective-permute-start.11 = (bf16[128,1408]{1,0:T(8,128)(2,1)}, bf16[128,1408]{1,0:T(8,128)(2,1)S(1)}, u32[]{:S(2)}, u32[]{:S(2)}) collective-permute-start(bf16[128,1408]{1,0:T(8,128)(2,1)} %get-tuple-element.62), channel_id=1, source_target_pairs={{0,17},{1,16},{2,19},{3,18},{4,21},{5,20},{6,23},{7,22},{8,25},{9,... | collective-permute-start | bytes 1081352 | tf_op jit(solution)/shard_map/ppermute | solution.py:55
  19.4 14.4 %collective-permute-start.5 = (bf16[4,128,256]{2,1,0:T(8,128)(2,1)S(1)}, bf16[4,128,256]{2,1,0:T(8,128)(2,1)S(1)}, u32[]{:S(2)}, u32[]{:S(2)}) collective-permute-start(bf16[4,128,256]{2,1,0:T(8,128)(2,1)S(1)} %collective-permute-done.4.refs_3_), channel_id=1, source_target_pairs={{0,14},{1,3},{2,0},{3,5},{4,2},{5,7},{6,4},{7,9},{8,6},{9,11},{10,... | collective-permute-start | bytes 786440 | tf_op jit(solution)/shard_map/ppermute | solution.py:55
  21.2 12.6 %collective-permute-start.7 = (bf16[4,128,256]{2,1,0:T(8,128)(2,1)S(1)}, bf16[4,128,256]{2,1,0:T(8,128)(2,1)S(1)}, u32[]{:S(2)}, u32[]{:S(2)}) collective-permute-start(bf16[4,128,256]{2,1,0:T(8,128)(2,1)S(1)} %collective-permute-done.6.refs_4_), channel_id=1, source_target_pairs={{0,2},{1,15},{2,4},{3,1},{4,6},{5,3},{6,8},{7,5},{8,10},{9,7},{10,... | collective-permute-start | bytes 786440 | tf_op jit(solution)/shard_map/ppermute | solution.py:55
  24.8 1.0 %copy-start = (bf16[128,1408]{1,0:T(8,128)(2,1)S(1)}, bf16[128,1408]{1,0:T(8,128)(2,1)}, u32[]{:S(2)}) copy-start(bf16[128,1408]{1,0:T(8,128)(2,1)} %get-tuple-element.52.refs_1_) | copy-start | bytes 1081348
  33.8 8.0 %collective-permute-start.9 = (bf16[4,128,256]{2,1,0:T(8,128)(2,1)S(1)}, bf16[4,128,256]{2,1,0:T(8,128)(2,1)S(1)}, u32[]{:S(2)}, u32[]{:S(2)}) collective-permute-start(bf16[4,128,256]{2,1,0:T(8,128)(2,1)S(1)} %collective-permute-done.7.refs_6_.refs_3_), channel_id=1, source_target_pairs={{0,2},{1,15},{2,4},{3,1},{4,6},{5,3},{6,8},{7,5},{8,10},{9,7},{10,... | collective-permute-start | bytes 786440 | tf_op jit(solution)/shard_map/ppermute | solution.py:55
  35.5 9.3 %collective-permute-start.8 = (bf16[4,128,256]{2,1,0:T(8,128)(2,1)S(1)}, bf16[4,128,256]{2,1,0:T(8,128)(2,1)S(1)}, u32[]{:S(2)}, u32[]{:S(2)}) collective-permute-start(bf16[4,128,256]{2,1,0:T(8,128)(2,1)S(1)} %collective-permute-done.5.refs_5_.refs_2_), channel_id=1, source_target_pairs={{0,14},{1,3},{2,0},{3,5},{4,2},{5,7},{6,4},{7,9},{8,6},{9,11},{10,... | collective-permute-start | bytes 786440 | tf_op jit(solution)/shard_map/ppermute | solution.py:55
  41.8 6.4 %collective-permute-start.12 = (bf16[4,128,256]{2,1,0:T(8,128)(2,1)S(1)}, bf16[4,128,256]{2,1,0:T(8,128)(2,1)S(1)}, u32[]{:S(2)}, u32[]{:S(2)}) collective-permute-start(bf16[4,128,256]{2,1,0:T(8,128)(2,1)S(1)} %collective-permute-done.9.refs_3_.refs_5_), channel_id=1, source_target_pairs={{0,2},{1,15},{2,4},{3,1},{4,6},{5,3},{6,8},{7,5},{8,10},{9,7},{10,... | collective-permute-start | bytes 786440 | tf_op jit(solution)/shard_map/ppermute | solution.py:55
  48.0 8.5 %copy-start.1 = (bf16[128,1408]{1,0:T(8,128)(2,1)S(1)}, bf16[128,1408]{1,0:T(8,128)(2,1)}, u32[]{:S(2)}) copy-start(bf16[128,1408]{1,0:T(8,128)(2,1)} %get-tuple-element.52.refs_1_) | copy-start | bytes 1081348
  50.5 12.8 %collective-permute-start.15 = (bf16[128,1024]{1,0:T(8,128)(2,1)S(1)}, bf16[128,1024]{1,0:T(8,128)(2,1)S(1)}, u32[]{:S(2)}, u32[]{:S(2)}) collective-permute-start(bf16[128,1024]{1,0:T(8,128)(2,1)S(1)} %get-tuple-element.78), channel_id=1, source_target_pairs={{0,16},{1,17},{2,18},{3,19},{4,20},{5,21},{6,22},{7,23},{8,24},{9,... | collective-permute-start | bytes 786440 | tf_op jit(solution)/shard_map/ppermute | solution.py:55
  52.6 13.4 %collective-permute-start.16 = (bf16[128,1024]{1,0:T(8,128)(2,1)S(1)}, bf16[128,1024]{1,0:T(8,128)(2,1)S(1)}, u32[]{:S(2)}, u32[]{:S(2)}) collective-permute-start(bf16[128,1024]{1,0:T(8,128)(2,1)S(1)} %get-tuple-element.72), channel_id=1, source_target_pairs={{0,17},{1,16},{2,19},{3,18},{4,21},{5,20},{6,23},{7,22},{8,25},{9,... | collective-permute-start | bytes 786440 | tf_op jit(solution)/shard_map/ppermute | solution.py:55
  61.6 1.4 %collective-permute-start.13 = (bf16[64,1024]{1,0:T(8,128)(2,1)S(1)}, bf16[64,1024]{1,0:T(8,128)(2,1)S(1)}, u32[]{:S(2)}, u32[]{:S(2)}) collective-permute-start(bf16[64,1024]{1,0:T(8,128)(2,1)S(1)} %get-tuple-element.76), channel_id=1, source_target_pairs={{0,1},{1,0},{2,3},{3,2},{4,5},{5,4},{6,7},{7,6},{8,9},{9,8},{10,11... | collective-permute-start | bytes 393224 | tf_op jit(solution)/shard_map/ppermute | solution.py:55
  62.0 1.3 %collective-permute-start.14 = (bf16[64,1024]{1,0:T(8,128)(2,1)S(1)}, bf16[64,1024]{1,0:T(8,128)(2,1)S(1)}, u32[]{:S(2)}, u32[]{:S(2)}) collective-permute-start(bf16[64,1024]{1,0:T(8,128)(2,1)S(1)} %get-tuple-element.77), channel_id=1, source_target_pairs={{0,1},{1,0},{2,3},{3,2},{4,5},{5,4},{6,7},{7,6},{8,9},{9,8},{10,11... | collective-permute-start | bytes 393224 | tf_op jit(solution)/shard_map/ppermute | solution.py:55

commit v3 on v2

--- a/solution.py
+++ b/solution.py
@@ -322,7 +322,8 @@
         return order * 4 + (table // 16 ^ x) * 2 + (table % 2 ^ c), lengths
 
     near, far = msgs[1::-1], msgs[2:]
-    near_work, far_work = entries(near), entries(far)
+    slots, lengths = entries([*near, *far])
+    near_work, far_work = (slots[:2], lengths[:2]), (slots[2:], lengths[2:])
     a, b = [piece], [piece]
     for _ in range(2):
         a.append(send(a[-1], AHEAD))

time: 67.4 us -> 70.2 us (1.042)
  Pallas kernels: 25.6 us -> 28.5 us
  waiting for transfers between devices: 11.5 us -> 12.9 us
  starting transfers between devices: 26.1 us -> 25.1 us
    pallas_call x5, Pallas kernels: 19.7 us -> 22.7 us  [run_attend(): pl.pallas_call(functools.partial(attend, low, high, not state, cuts), out...]
    ppermute x17, waiting for transfers between devices: 11.5 us -> 12.9 us  [send(): return lax.ppermute(piece, 'blk', table)]
    ppermute x17, starting transfers between devices: 26.1 us -> 25.1 us  [send(): return lax.ppermute(piece, 'blk', table)]
  transfers between devices with their start and end apart: 17 -> 17, of which waited for: 8 -> 6; matrix products, arithmetic and copies ran while one was open for 3% -> 3% of each run, Pallas kernels for 31% -> 32%
where the time goes in v3:
time: 70.2 us; the launch traced here: 70.3 us
  Pallas kernels  28.5 us (41%)
  starting transfers between devices  25.1 us (36%)
  waiting for transfers between devices  12.9 us (18%)
  local copies, waits for them, and re-layouts  1.89 us (3%)
  between operations  1.01 us (1%)
  other arithmetic  0.92 us (1%)
    ppermute x17, starting transfers between devices, send(): return lax.ppermute(piece, 'blk', table)  25.1 us
    pallas_call x5, Pallas kernels, run_attend(): pl.pallas_call(functools.partial(attend, low, high, not state, cuts), out...  22.7 us
    ppermute x17, waiting for transfers between devices, send(): return lax.ppermute(piece, 'blk', table)  12.9 us
    pallas_call x1, Pallas kernels, body(): pl.pallas_call(pack_request, out_shape=[jax.ShapeDtypeStruct((BS, MSG), j...  3.17 us
    pallas_call x1, Pallas kernels, body(): pl.pallas_call(pack_pool, out_shape=[jax.ShapeDtypeStruct((BS, 2 * DH), j...  1.64 us
  transfers between devices with their start and end apart: 17, of which 6 were waited for; matrix products, arithmetic and copies ran while one was open for 3% of the time, Pallas kernels for 32%

profile of v3, /device:TPU:1, one launch (start us, length us, event | category | flops | bytes accessed | tf_op | source)
XLA Modules:
  0.0 70.3 jit_solution(9756036018062647569)
XLA Ops:
  0.0 1.6 %shard_map.73 = (bf16[128,256]{1,0:T(8,128)(2,1)}, bf16[128,256]{1,0:T(8,128)(2,1)}, bf16[128,256]{1,0:T(8,128)(2,1)}, bf16[128,256]{1,0:T(8,128)(2,1)}) custom-call(bf16[128,512]{1,0:T(8,128)(2,1)} %k_ref.2, bf16[128,512]{1,0:T(8,128)(2,1)} %v_ref.2), custom_call_target="tpu_custom_call" | custom-call | tf_op jit(solution)/shard_map/pallas_call | solution.py:293
  1.7 3.3 %collective-permute-start = (bf16[128,256]{1,0:T(8,128)(2,1)}, bf16[128,256]{1,0:T(8,128)(2,1)S(1)}, u32[]{:S(2)}, u32[]{:S(2)}) collective-permute-start(bf16[128,256]{1,0:T(8,128)(2,1)} %get-tuple-element.43), channel_id=1, source_target_pairs={{0,1},{1,0},{2,3},{3,2},{4,5},{5,4},{6,7},{7,6},{8,9},{9,8},{10,11... | collective-permute-start | bytes 196616 | tf_op jit(solution)/shard_map/ppermute | solution.py:55
  5.0 1.7 %collective-permute-start.2 = (bf16[128,256]{1,0:T(8,128)(2,1)}, bf16[128,256]{1,0:T(8,128)(2,1)S(1)}, u32[]{:S(2)}, u32[]{:S(2)}) collective-permute-start(bf16[128,256]{1,0:T(8,128)(2,1)} %get-tuple-element.45), channel_id=1, source_target_pairs={{0,17},{1,16},{2,19},{3,18},{4,21},{5,20},{6,23},{7,22},{8,25},{9,... | collective-permute-start | bytes 196616 | tf_op jit(solution)/shard_map/ppermute | solution.py:55
  7.4 3.2 %shard_map.74 = (bf16[128,1408]{1,0:T(8,128)(2,1)}, bf16[128,1408]{1,0:T(8,128)(2,1)}, bf16[128,1408]{1,0:T(8,128)(2,1)}, bf16[128,1408]{1,0:T(8,128)(2,1)}) custom-call(s32[1,16]{1,0:T(1,128)} %table_ref.1, s32[1]{0:T(128)S(6)} %copy.8.length_ref, bf16[128,4096]{1,0:T(8,128)(2,1)} %q_ref, bf16[128,512]{1,0:T(8,128)(2,1)} %k_ref.3, bf16[128,512]{1,0:T(8,128)(2,1)} %v_ref.3), custom_call_target="tpu_custom_call" | custom-call | flops 1 | bytes 1 | tf_op jit(solution)/shard_map/pallas_call | solution.py:301
  10.6 0.2 collective-permute-start.4
  10.7 1.7 %collective-permute-start.5 = (bf16[128,1408]{1,0:T(8,128)(2,1)}, bf16[128,1408]{1,0:T(8,128)(2,1)S(1)}, u32[]{:S(2)}, u32[]{:S(2)}) collective-permute-start(bf16[128,1408]{1,0:T(8,128)(2,1)} %get-tuple-element.54), channel_id=1, source_target_pairs={{0,17},{1,16},{2,19},{3,18},{4,21},{5,20},{6,23},{7,22},{8,25},{9,... | collective-permute-start | bytes 1081352 | tf_op jit(solution)/shard_map/ppermute | solution.py:55
  12.5 0.1 collective-permute-start.3
  12.5 0.9 %pad_maximum_fusion.refs_2_ = bf16[4,128,256]{2,1,0:T(8,128)(2,1)S(1)} fusion(bf16[1,128,256]{2,1,0:T(8,128)(2,1)S(1)} %bitcast.7, bf16[1,128,256]{2,1,0:T(8,128)(2,1)S(1)} %bitcast.6, bf16[1,128,256]{2,1,0:T(8,128)(2,1)S(1)} %bitcast.5, bf16[1,128,256]{2,1,0:T(8,128)(2,1)} %bitcast.4), kind=kLoop, calls=%fused_computation | loop fusion | flops 393216 | bytes 524288 | tf_op jit(solution)/shard_map/stack | solution.py:311
  13.4 0.1 collective-permute-start.6
  13.5 3.9 %collective-permute-start.8 = (bf16[4,128,256]{2,1,0:T(8,128)(2,1)S(1)}, bf16[4,128,256]{2,1,0:T(8,128)(2,1)S(1)}, u32[]{:S(2)}, u32[]{:S(2)}) collective-permute-start(bf16[4,128,256]{2,1,0:T(8,128)(2,1)S(1)} %pad_maximum_fusion.refs_2_), channel_id=1, source_target_pairs={{0,2},{1,15},{2,4},{3,1},{4,6},{5,3},{6,8},{7,5},{8,10},{9,7},{10,... | collective-permute-start | bytes 786440 | tf_op jit(solution)/shard_map/ppermute | solution.py:55
  17.4 0.7 slice.37
  18.1 3.0 %collective-permute-done.6.refs_3_ = bf16[4,128,256]{2,1,0:T(8,128)(2,1)S(1)} collective-permute-done((bf16[4,128,256]{2,1,0:T(8,128)(2,1)S(1)}, bf16[4,128,256]{2,1,0:T(8,128)(2,1)S(1)}, u32[]{:S(2)}, u32[]{:S(2)}) %collective-permute-start.6) | collective-permute-done | bytes 262176 | tf_op jit(solution)/shard_map/ppermute | solution.py:55
  21.1 1.6 %collective-permute-done.8.refs_4_ = bf16[4,128,256]{2,1,0:T(8,128)(2,1)S(1)} collective-permute-done((bf16[4,128,256]{2,1,0:T(8,128)(2,1)S(1)}, bf16[4,128,256]{2,1,0:T(8,128)(2,1)S(1)}, u32[]{:S(2)}, u32[]{:S(2)}) %collective-permute-start.8) | collective-permute-done | bytes 262176 | tf_op jit(solution)/shard_map/ppermute | solution.py:55
  22.7 3.4 %collective-permute-start.9 = (bf16[4,128,256]{2,1,0:T(8,128)(2,1)S(1)}, bf16[4,128,256]{2,1,0:T(8,128)(2,1)S(1)}, u32[]{:S(2)}, u32[]{:S(2)}) collective-permute-start(bf16[4,128,256]{2,1,0:T(8,128)(2,1)S(1)} %collective-permute-done.8.refs_4_), channel_id=1, source_target_pairs={{0,2},{1,15},{2,4},{3,1},{4,6},{5,3},{6,8},{7,5},{8,10},{9,7},{10,... | collective-permute-start | bytes 786440 | tf_op jit(solution)/shard_map/ppermute | solution.py:55
  26.1 2.9 %collective-permute-done.5.refs_1_ = bf16[128,1408]{1,0:T(8,128)(2,1)S(1)} collective-permute-done((bf16[128,1408]{1,0:T(8,128)(2,1)}, bf16[128,1408]{1,0:T(8,128)(2,1)S(1)}, u32[]{:S(2)}, u32[]{:S(2)}) %collective-permute-start.5) | collective-permute-done | bytes 360480 | tf_op jit(solution)/shard_map/ppermute | solution.py:55
  29.1 0.2 slice_reduce_fusion
  29.3 1.0 %copy-done = bf16[128,1408]{1,0:T(8,128)(2,1)S(1)} copy-done((bf16[128,1408]{1,0:T(8,128)(2,1)S(1)}, bf16[128,1408]{1,0:T(8,128)(2,1)}, u32[]{:S(2)}) %copy-start) | copy-done | bytes 360472
  30.3 3.7 %shard_map.75 = (f32[2,1024,128]{2,1,0:T(8,128)S(1)}, f32[2,1024,256]{2,1,0:T(8,128)S(1)}) custom-call(s32[2,16]{1,0:T(2,128)S(1)} %get-tuple-element.82.slot_ref, s32[2]{0:T(128)S(1)} %get-tuple-element.80.length_ref, bf16[128,1408]{1,0:T(8,128)(2,1)S(1)} %collective-permute-done.3.refs_0_, bf16[128,1408]{1,0:T(8,128)(2,1)S(1)} %copy-done, ...), custom_call_target="tpu_custom_call" | custom-call | flops 1 | bytes 1 | tf_op jit(solution)/shard_map/pallas_call | solution.py:272
  34.1 4.7 %collective-permute-start.11 = (bf16[4,128,256]{2,1,0:T(8,128)(2,1)S(1)}, bf16[4,128,256]{2,1,0:T(8,128)(2,1)S(1)}, u32[]{:S(2)}, u32[]{:S(2)}) collective-permute-start(bf16[4,128,256]{2,1,0:T(8,128)(2,1)S(1)} %collective-permute-done.9.refs_6_.refs_3_), channel_id=1, source_target_pairs={{0,2},{1,15},{2,4},{3,1},{4,6},{5,3},{6,8},{7,5},{8,10},{9,7},{10,... | collective-permute-start | bytes 786440 | tf_op jit(solution)/shard_map/ppermute | solution.py:55
  38.8 6.5 %shard_map.76 = (f32[2,1024,128]{2,1,0:T(8,128)S(1)}, f32[2,1024,256]{2,1,0:T(8,128)S(1)}) custom-call(s32[2,16]{1,0:T(2,128)S(1)} %get-tuple-element.81.slot_ref, s32[2]{0:T(128)S(1)} %get-tuple-element.79.length_ref, bf16[128,1408]{1,0:T(8,128)(2,1)S(1)} %collective-permute-done.4.refs_0_, bf16[128,1408]{1,0:T(8,128)(2,1)S(1)} %collective-permute-done.5.refs_1_, ...), custom_call_target="tpu_custom_call" | custom-call | flops 1 | bytes 1 | tf_op jit(solution)/shard_map/pallas_call | solution.py:272
  45.3 2.7 %collective-permute-start.12 = (bf16[4,128,256]{2,1,0:T(8,128)(2,1)S(1)}, bf16[4,128,256]{2,1,0:T(8,128)(2,1)S(1)}, u32[]{:S(2)}, u32[]{:S(2)}) collective-permute-start(bf16[4,128,256]{2,1,0:T(8,128)(2,1)S(1)} %collective-permute-done.11.refs_3_.refs_5_), channel_id=1, source_target_pairs={{0,2},{1,15},{2,4},{3,1},{4,6},{5,3},{6,8},{7,5},{8,10},{9,7},{10,... | collective-permute-start | bytes 786440 | tf_op jit(solution)/shard_map/ppermute | solution.py:55
  48.0 4.1 %shard_map.77 = (f32[2,1024,128]{2,1,0:T(8,128)S(1)}, f32[2,1024,256]{2,1,0:T(8,128)S(1)}) custom-call(s32[2,16]{1,0:T(2,128)S(1)} %get-tuple-element.81.slot_ref, s32[2]{0:T(128)S(1)} %get-tuple-element.79.length_ref, bf16[128,1408]{1,0:T(8,128)(2,1)S(1)} %collective-permute-done.4.refs_0_, bf16[128,1408]{1,0:T(8,128)(2,1)S(1)} %collective-permute-done.5.refs_1_, ...), custom_call_target="tpu_custom_call" | custom-call | flops 1 | bytes 1 | tf_op jit(solution)/shard_map/pallas_call | solution.py:272
  52.2 3.2 %shard_map.78 = (bf16[128,1024]{1,0:T(8,128)(2,1)S(1)}, bf16[128,1024]{1,0:T(8,128)(2,1)S(1)}) custom-call(s32[2,16]{1,0:T(2,128)S(1)} %get-tuple-element.81.slot_ref, s32[2]{0:T(128)S(1)} %get-tuple-element.79.length_ref, bf16[128,1408]{1,0:T(8,128)(2,1)S(1)} %collective-permute-done.4.refs_0_, bf16[128,1408]{1,0:T(8,128)(2,1)S(1)} %collective-permute-done.5.refs_1_, ...), custom_call_target="tpu_custom_call" | custom-call | flops 1 | bytes 1 | tf_op jit(solution)/shard_map/pallas_call | solution.py:272
  55.4 0.1 collective-permute-start.15
  55.5 2.5 %collective-permute-start.16 = (bf16[128,1024]{1,0:T(8,128)(2,1)S(1)}, bf16[128,1024]{1,0:T(8,128)(2,1)S(1)}, u32[]{:S(2)}, u32[]{:S(2)}) collective-permute-start(bf16[128,1024]{1,0:T(8,128)(2,1)S(1)} %get-tuple-element.72), channel_id=1, source_target_pairs={{0,17},{1,16},{2,19},{3,18},{4,21},{5,20},{6,23},{7,22},{8,25},{9,... | collective-permute-start | bytes 786440 | tf_op jit(solution)/shard_map/ppermute | solution.py:55
  58.0 5.2 %shard_map.79 = (bf16[64,1024]{1,0:T(8,128)(2,1)S(1)}, bf16[64,1024]{1,0:T(8,128)(2,1)S(1)}, bf16[128,1024]{1,0:T(8,128)(2,1)S(1)}) custom-call(s32[2,16]{1,0:T(2,128)S(1)} %get-tuple-element.82.slot_ref, s32[2]{0:T(128)S(1)} %get-tuple-element.80.length_ref, bf16[128,1408]{1,0:T(8,128)(2,1)S(1)} %collective-permute-done.3.refs_0_, ...), custom_call_target="tpu_custom_call" | custom-call | flops 1 | bytes 1 | tf_op jit(solution)/shard_map/pallas_call | solution.py:272
  63.2 0.1 collective-permute-start.13
  63.3 0.5 collective-permute-start.14
  63.8 0.8 %collective-permute-done.13.refs_1_ = bf16[64,1024]{1,0:T(8,128)(2,1)S(1)} collective-permute-done((bf16[64,1024]{1,0:T(8,128)(2,1)S(1)}, bf16[64,1024]{1,0:T(8,128)(2,1)S(1)}, u32[]{:S(2)}, u32[]{:S(2)}) %collective-permute-start.13) | collective-permute-done | bytes 131104 | tf_op jit(solution)/shard_map/ppermute | solution.py:55
  64.6 0.2 collective-permute-done.14.refs_2_
  64.8 4.3 %collective-permute-done.16.refs_4_ = bf16[128,1024]{1,0:T(8,128)(2,1)S(1)} collective-permute-done((bf16[128,1024]{1,0:T(8,128)(2,1)S(1)}, bf16[128,1024]{1,0:T(8,128)(2,1)S(1)}, u32[]{:S(2)}, u32[]{:S(2)}) %collective-permute-start.16) | collective-permute-done | bytes 262176 | tf_op jit(solution)/shard_map/ppermute | solution.py:55
  69.1 1.0 %shard_map.80 = bf16[128,4096]{1,0:T(8,128)(2,1)} custom-call(bf16[128,1024]{1,0:T(8,128)(2,1)S(1)} %get-tuple-element.75.refs_0_, bf16[64,1024]{1,0:T(8,128)(2,1)S(1)} %collective-permute-done.13.refs_1_, bf16[64,1024]{1,0:T(8,128)(2,1)S(1)} %collective-permute-done.14.refs_2_, bf16[128,1024]{1,0:T(8,128)(2,1)S(1)} %collective-permute-done.15.refs_3_, ...), custom_call_target="tpu_custom_call" | custom-call | tf_op jit(solution)/shard_map/pallas_call | solution.py:349
  (23 shorter events, 0.1 us)
Async XLA Ops:
  1.7 8.9 %collective-permute-start = (bf16[128,256]{1,0:T(8,128)(2,1)}, bf16[128,256]{1,0:T(8,128)(2,1)S(1)}, u32[]{:S(2)}, u32[]{:S(2)}) collective-permute-start(bf16[128,256]{1,0:T(8,128)(2,1)} %get-tuple-element.43), channel_id=1, source_target_pairs={{0,1},{1,0},{2,3},{3,2},{4,5},{5,4},{6,7},{7,6},{8,9},{9,8},{10,11... | collective-permute-start | bytes 196616 | tf_op jit(solution)/shard_map/ppermute | solution.py:55
  5.0 5.6 %collective-permute-start.1 = (bf16[128,256]{1,0:T(8,128)(2,1)}, bf16[128,256]{1,0:T(8,128)(2,1)S(1)}, u32[]{:S(2)}, u32[]{:S(2)}) collective-permute-start(bf16[128,256]{1,0:T(8,128)(2,1)} %get-tuple-element.44), channel_id=1, source_target_pairs={{0,16},{1,17},{2,18},{3,19},{4,20},{5,21},{6,22},{7,23},{8,24},{9,... | collective-permute-start | bytes 196616 | tf_op jit(solution)/shard_map/ppermute | solution.py:55
  5.0 5.6 %collective-permute-start.2 = (bf16[128,256]{1,0:T(8,128)(2,1)}, bf16[128,256]{1,0:T(8,128)(2,1)S(1)}, u32[]{:S(2)}, u32[]{:S(2)}) collective-permute-start(bf16[128,256]{1,0:T(8,128)(2,1)} %get-tuple-element.45), channel_id=1, source_target_pairs={{0,17},{1,16},{2,19},{3,18},{4,21},{5,20},{6,23},{7,22},{8,25},{9,... | collective-permute-start | bytes 196616 | tf_op jit(solution)/shard_map/ppermute | solution.py:55
  10.6 15.6 %collective-permute-start.4 = (bf16[128,1408]{1,0:T(8,128)(2,1)}, bf16[128,1408]{1,0:T(8,128)(2,1)S(1)}, u32[]{:S(2)}, u32[]{:S(2)}) collective-permute-start(bf16[128,1408]{1,0:T(8,128)(2,1)} %get-tuple-element.53), channel_id=1, source_target_pairs={{0,16},{1,17},{2,18},{3,19},{4,20},{5,21},{6,22},{7,23},{8,24},{9,... | collective-permute-start | bytes 1081352 | tf_op jit(solution)/shard_map/ppermute | solution.py:55
  10.7 18.3 %collective-permute-start.5 = (bf16[128,1408]{1,0:T(8,128)(2,1)}, bf16[128,1408]{1,0:T(8,128)(2,1)S(1)}, u32[]{:S(2)}, u32[]{:S(2)}) collective-permute-start(bf16[128,1408]{1,0:T(8,128)(2,1)} %get-tuple-element.54), channel_id=1, source_target_pairs={{0,17},{1,16},{2,19},{3,18},{4,21},{5,20},{6,23},{7,22},{8,25},{9,... | collective-permute-start | bytes 1081352 | tf_op jit(solution)/shard_map/ppermute | solution.py:55
  12.5 16.6 %collective-permute-start.3 = (bf16[128,1408]{1,0:T(8,128)(2,1)}, bf16[128,1408]{1,0:T(8,128)(2,1)S(1)}, u32[]{:S(2)}, u32[]{:S(2)}) collective-permute-start(bf16[128,1408]{1,0:T(8,128)(2,1)} %get-tuple-element.51), channel_id=1, source_target_pairs={{0,1},{1,0},{2,3},{3,2},{4,5},{5,4},{6,7},{7,6},{8,9},{9,8},{10,11... | collective-permute-start | bytes 1081352 | tf_op jit(solution)/shard_map/ppermute | solution.py:55
  13.4 7.7 %collective-permute-start.6 = (bf16[4,128,256]{2,1,0:T(8,128)(2,1)S(1)}, bf16[4,128,256]{2,1,0:T(8,128)(2,1)S(1)}, u32[]{:S(2)}, u32[]{:S(2)}) collective-permute-start(bf16[4,128,256]{2,1,0:T(8,128)(2,1)S(1)} %pad_maximum_fusion.refs_2_), channel_id=1, source_target_pairs={{0,14},{1,3},{2,0},{3,5},{4,2},{5,7},{6,4},{7,9},{8,6},{9,11},{10,... | collective-permute-start | bytes 786440 | tf_op jit(solution)/shard_map/ppermute | solution.py:55
  13.5 9.2 %collective-permute-start.8 = (bf16[4,128,256]{2,1,0:T(8,128)(2,1)S(1)}, bf16[4,128,256]{2,1,0:T(8,128)(2,1)S(1)}, u32[]{:S(2)}, u32[]{:S(2)}) collective-permute-start(bf16[4,128,256]{2,1,0:T(8,128)(2,1)S(1)} %pad_maximum_fusion.refs_2_), channel_id=1, source_target_pairs={{0,2},{1,15},{2,4},{3,1},{4,6},{5,3},{6,8},{7,5},{8,10},{9,7},{10,... | collective-permute-start | bytes 786440 | tf_op jit(solution)/shard_map/ppermute | solution.py:55
  21.1 13.0 %collective-permute-start.7 = (bf16[4,128,256]{2,1,0:T(8,128)(2,1)S(1)}, bf16[4,128,256]{2,1,0:T(8,128)(2,1)S(1)}, u32[]{:S(2)}, u32[]{:S(2)}) collective-permute-start(bf16[4,128,256]{2,1,0:T(8,128)(2,1)S(1)} %collective-permute-done.6.refs_3_), channel_id=1, source_target_pairs={{0,14},{1,3},{2,0},{3,5},{4,2},{5,7},{6,4},{7,9},{8,6},{9,11},{10,... | collective-permute-start | bytes 786440 | tf_op jit(solution)/shard_map/ppermute | solution.py:55
  22.7 11.4 %collective-permute-start.9 = (bf16[4,128,256]{2,1,0:T(8,128)(2,1)S(1)}, bf16[4,128,256]{2,1,0:T(8,128)(2,1)S(1)}, u32[]{:S(2)}, u32[]{:S(2)}) collective-permute-start(bf16[4,128,256]{2,1,0:T(8,128)(2,1)S(1)} %collective-permute-done.8.refs_4_), channel_id=1, source_target_pairs={{0,2},{1,15},{2,4},{3,1},{4,6},{5,3},{6,8},{7,5},{8,10},{9,7},{10,... | collective-permute-start | bytes 786440 | tf_op jit(solution)/shard_map/ppermute | solution.py:55
  29.3 1.0 %copy-start = (bf16[128,1408]{1,0:T(8,128)(2,1)S(1)}, bf16[128,1408]{1,0:T(8,128)(2,1)}, u32[]{:S(2)}) copy-start(bf16[128,1408]{1,0:T(8,128)(2,1)} %get-tuple-element.52.refs_1_) | copy-start | bytes 1081348
  34.1 11.2 %collective-permute-start.11 = (bf16[4,128,256]{2,1,0:T(8,128)(2,1)S(1)}, bf16[4,128,256]{2,1,0:T(8,128)(2,1)S(1)}, u32[]{:S(2)}, u32[]{:S(2)}) collective-permute-start(bf16[4,128,256]{2,1,0:T(8,128)(2,1)S(1)} %collective-permute-done.9.refs_6_.refs_3_), channel_id=1, source_target_pairs={{0,2},{1,15},{2,4},{3,1},{4,6},{5,3},{6,8},{7,5},{8,10},{9,7},{10,... | collective-permute-start | bytes 786440 | tf_op jit(solution)/shard_map/ppermute | solution.py:55
  38.8 9.2 %collective-permute-start.10 = (bf16[4,128,256]{2,1,0:T(8,128)(2,1)S(1)}, bf16[4,128,256]{2,1,0:T(8,128)(2,1)S(1)}, u32[]{:S(2)}, u32[]{:S(2)}) collective-permute-start(bf16[4,128,256]{2,1,0:T(8,128)(2,1)S(1)} %collective-permute-done.7.refs_5_.refs_2_), channel_id=1, source_target_pairs={{0,14},{1,3},{2,0},{3,5},{4,2},{5,7},{6,4},{7,9},{8,6},{9,11},{10,... | collective-permute-start | bytes 786440 | tf_op jit(solution)/shard_map/ppermute | solution.py:55
  45.3 6.9 %collective-permute-start.12 = (bf16[4,128,256]{2,1,0:T(8,128)(2,1)S(1)}, bf16[4,128,256]{2,1,0:T(8,128)(2,1)S(1)}, u32[]{:S(2)}, u32[]{:S(2)}) collective-permute-start(bf16[4,128,256]{2,1,0:T(8,128)(2,1)S(1)} %collective-permute-done.11.refs_3_.refs_5_), channel_id=1, source_target_pairs={{0,2},{1,15},{2,4},{3,1},{4,6},{5,3},{6,8},{7,5},{8,10},{9,7},{10,... | collective-permute-start | bytes 786440 | tf_op jit(solution)/shard_map/ppermute | solution.py:55
  52.2 5.8 %copy-start.1 = (bf16[128,1408]{1,0:T(8,128)(2,1)S(1)}, bf16[128,1408]{1,0:T(8,128)(2,1)}, u32[]{:S(2)}) copy-start(bf16[128,1408]{1,0:T(8,128)(2,1)} %get-tuple-element.52.refs_1_) | copy-start | bytes 1081348
  55.4 9.4 %collective-permute-start.15 = (bf16[128,1024]{1,0:T(8,128)(2,1)S(1)}, bf16[128,1024]{1,0:T(8,128)(2,1)S(1)}, u32[]{:S(2)}, u32[]{:S(2)}) collective-permute-start(bf16[128,1024]{1,0:T(8,128)(2,1)S(1)} %get-tuple-element.78), channel_id=1, source_target_pairs={{0,16},{1,17},{2,18},{3,19},{4,20},{5,21},{6,22},{7,23},{8,24},{9,... | collective-permute-start | bytes 786440 | tf_op jit(solution)/shard_map/ppermute | solution.py:55
  55.5 13.6 %collective-permute-start.16 = (bf16[128,1024]{1,0:T(8,128)(2,1)S(1)}, bf16[128,1024]{1,0:T(8,128)(2,1)S(1)}, u32[]{:S(2)}, u32[]{:S(2)}) collective-permute-start(bf16[128,1024]{1,0:T(8,128)(2,1)S(1)} %get-tuple-element.72), channel_id=1, source_target_pairs={{0,17},{1,16},{2,19},{3,18},{4,21},{5,20},{6,23},{7,22},{8,25},{9,... | collective-permute-start | bytes 786440 | tf_op jit(solution)/shard_map/ppermute | solution.py:55
  63.2 1.4 %collective-permute-start.13 = (bf16[64,1024]{1,0:T(8,128)(2,1)S(1)}, bf16[64,1024]{1,0:T(8,128)(2,1)S(1)}, u32[]{:S(2)}, u32[]{:S(2)}) collective-permute-start(bf16[64,1024]{1,0:T(8,128)(2,1)S(1)} %get-tuple-element.76), channel_id=1, source_target_pairs={{0,1},{1,0},{2,3},{3,2},{4,5},{5,4},{6,7},{7,6},{8,9},{9,8},{10,11... | collective-permute-start | bytes 393224 | tf_op jit(solution)/shard_map/ppermute | solution.py:55
  63.3 1.5 %collective-permute-start.14 = (bf16[64,1024]{1,0:T(8,128)(2,1)S(1)}, bf16[64,1024]{1,0:T(8,128)(2,1)S(1)}, u32[]{:S(2)}, u32[]{:S(2)}) collective-permute-start(bf16[64,1024]{1,0:T(8,128)(2,1)S(1)} %get-tuple-element.77), channel_id=1, source_target_pairs={{0,1},{1,0},{2,3},{3,2},{4,5},{5,4},{6,7},{7,6},{8,9},{9,8},{10,11... | collective-permute-start | bytes 393224 | tf_op jit(solution)/shard_map/ppermute | solution.py:55
